TPU v7x, 512 devices: a whole 4x8x8 slice. The times are simulated.
512 devices in a mesh: block: 32 (over z, x), tile: 16 (over y, core).
Axes of the slice: x: 4, y: 8, z: 8, core: 2. Of those that a mesh axis runs over, the one named last changes fastest.
Arguments:
- params: float32 [59, 262144], P(None, ('block', 'tile')), may hold values from -4 to 3, as said below
- moment1: float32 [59, 262144], P(None, ('block', 'tile')), may hold values from -0.6 to 0.6
- moment2: float32 [59, 262144], P(None, ('block', 'tile')), may hold values from 0.01 to 1
- tile_lists: int32 [512, 8, 256], P(('block', 'tile')), may hold values from -1 to 8191, as said below
- cameras: float32 [32, 2, 8], P('block'), may hold values from -0.4 to 170, as said below
- targets: float32 [512, 8, 3, 256], P(('block', 'tile')), may hold values from 0 to 1
- boundary_index: int32 [512, 2, 128], P(('block', 'tile')), may hold values from 0 to 511, as said below
- links: int32 [32], replicated, may hold values 0 or 1
- consensus: float32 [512, 2, 59, 128], P(('block', 'tile')), may hold values from -6 to 6
- duals: float32 [512, 2, 59, 128], P(('block', 'tile')), may hold values from -0.6 to 0.6
Outputs:
- params_out: float32 [59, 262144], P(None, ('block', 'tile'))
- moment1_out: float32 [59, 262144], P(None, ('block', 'tile'))
- moment2_out: float32 [59, 262144], P(None, ('block', 'tile'))
- consensus_out: float32 [512, 2, 59, 128], P(('block', 'tile'))
- duals_out: float32 [512, 2, 59, 128], P(('block', 'tile'))
Inputs may be any that keep to these rules, and one draw needn't show every extreme that they name: `params`: rows 0-2 lie in -1 to 1, rows 3-5 in -1 to 0, row 6 in 0.6 to 1.2, rows 7-9 in -1 to 1, row 10 in -4 to -1.5, rows 11 to 58 in -3 to 3. `cameras`: entries 0-3 are a quaternion whose first entry is 1 and others within -0.4 to 0.4, entries 4-5 lie in -0.3 to 0.3, entry 6 in 3.5 to 4.5, entry 7 in 130 to 170. `tile_lists`: -1 marks an empty slot; all empty slots of a list come after its live ones, and live entries stand in compositing order, front first. At most 16 live entries of one list are held by any one tile device, and in every list exactly 16 are held by some tile device. `boundary_index`: the 256 entries of one device are distinct. Entry [., 1, j] of device (b, t) and entry [., 0, j] of device (b + 1, t) are copies of one splat.
All inputs are finite; a program needn't handle non-finite values.
Results may differ from a plain program's by a relative error of at most 0.0003.
Values sent between devices are 32-bit elements; how exact they have to be, the bound alone decides.
No kernel may reach another device: no remote copies, remote signals or barrier semaphores. Data moves between devices by JAX's collectives and lax.ppermute only.
A program may use at most 64 MiB of HBM per device.

v0:
```python
import jax
import jax.numpy as jnp
from jax import lax
from jax.sharding import PartitionSpec as P

PARAMS = 59
SCREENS = 4
ROUNDS = 2
PIX = 256


sh_zero = 0.28209479177387814
sh_one = 0.4886025119029199
sh_two = (
    1.0925484305920792,
    -1.0925484305920792,
    0.31539156525252005,
    -1.0925484305920792,
    0.5462742152960396,
)
sh_three = (
    -0.5900435899266435,
    2.890611442640554,
    -0.4570457994644658,
    0.3731763325901154,
    -0.4570457994644658,
    1.445305721320277,
    -0.5900435899266435,
)
beta_one = 0.9
beta_two = 0.999
learn_rate = 0.01
adam_eps = 1e-08
penalty = 2.0
first_step = 100
blur_var = 0.3
opacity_cap = 0.99
highest = lax.Precision.HIGHEST


def shifted(x, axis, by):
    size = lax.axis_size(axis)
    pairs = [(i, i + by) for i in range(size) if 0 <= i + by < size]
    return lax.ppermute(x, axis, pairs)


def rotation(quat_w, quat_x, quat_y, quat_z):
    inverse = lax.rsqrt(quat_w * quat_w + quat_x * quat_x + quat_y * quat_y + quat_z * quat_z)
    unit_w = quat_w * inverse
    unit_x = quat_x * inverse
    unit_y = quat_y * inverse
    unit_z = quat_z * inverse
    return (
        (
            1.0 - 2.0 * (unit_y * unit_y + unit_z * unit_z),
            2.0 * (unit_x * unit_y - unit_w * unit_z),
            2.0 * (unit_x * unit_z + unit_w * unit_y),
        ),
        (
            2.0 * (unit_x * unit_y + unit_w * unit_z),
            1.0 - 2.0 * (unit_x * unit_x + unit_z * unit_z),
            2.0 * (unit_y * unit_z - unit_w * unit_x),
        ),
        (
            2.0 * (unit_x * unit_z - unit_w * unit_y),
            2.0 * (unit_y * unit_z + unit_w * unit_x),
            1.0 - 2.0 * (unit_x * unit_x + unit_y * unit_y),
        ),
    )


def sh_terms(dir_x, dir_y, dir_z):
    sq_x = dir_x * dir_x
    sq_y = dir_y * dir_y
    sq_z = dir_z * dir_z
    return (
        sh_zero + 0.0 * dir_x,
        -sh_one * dir_y,
        sh_one * dir_z,
        -sh_one * dir_x,
        sh_two[0] * dir_x * dir_y,
        sh_two[1] * dir_y * dir_z,
        sh_two[2] * (2.0 * sq_z - sq_x - sq_y),
        sh_two[3] * dir_x * dir_z,
        sh_two[4] * (sq_x - sq_y),
        sh_three[0] * dir_y * (3.0 * sq_x - sq_y),
        sh_three[1] * dir_x * dir_y * dir_z,
        sh_three[2] * dir_y * (4.0 * sq_z - sq_x - sq_y),
        sh_three[3] * dir_z * (2.0 * sq_z - 3.0 * sq_x - 3.0 * sq_y),
        sh_three[4] * dir_x * (4.0 * sq_z - sq_x - sq_y),
        sh_three[5] * dir_z * (sq_x - sq_y),
        sh_three[6] * dir_x * (sq_x - 3.0 * sq_y),
    )


def render_list(splats, live_mask, camera, pixel_x, pixel_y, centre_y, goal_img):
    cam_rot = rotation(camera[0], camera[1], camera[2], camera[3])
    shift_vec = (camera[4], camera[5], camera[6])
    focal_len = camera[7]
    centre = (splats[0], splats[1], splats[2])
    in_cam = [
        cam_rot[row_idx][0] * centre[0]
        + cam_rot[row_idx][1] * centre[1]
        + cam_rot[row_idx][2] * centre[2]
        + shift_vec[row_idx]
        for row_idx in range(3)
    ]
    inv_depth = 1.0 / in_cam[2]
    mean_x = focal_len * in_cam[0] * inv_depth + 64.0
    mean_y = focal_len * in_cam[1] * inv_depth + centre_y
    jacobian = (
        (focal_len * inv_depth, 0.0, -focal_len * in_cam[0] * inv_depth * inv_depth),
        (0.0, focal_len * inv_depth, -focal_len * in_cam[1] * inv_depth * inv_depth),
    )
    screen_map = [
        [
            jacobian[row_idx][0] * cam_rot[0][col_idx]
            + jacobian[row_idx][1] * cam_rot[1][col_idx]
            + jacobian[row_idx][2] * cam_rot[2][col_idx]
            for col_idx in range(3)
        ]
        for row_idx in range(2)
    ]
    local_rot = rotation(splats[6], splats[7], splats[8], splats[9])
    scales = [jnp.exp(splats[3 + col_idx]) for col_idx in range(3)]
    axes_flat = [
        [
            (
                screen_map[row_idx][0] * local_rot[0][col_idx]
                + screen_map[row_idx][1] * local_rot[1][col_idx]
                + screen_map[row_idx][2] * local_rot[2][col_idx]
            )
            * scales[col_idx]
            for col_idx in range(3)
        ]
        for row_idx in range(2)
    ]
    cov_xx = (
        axes_flat[0][0] * axes_flat[0][0]
        + axes_flat[0][1] * axes_flat[0][1]
        + axes_flat[0][2] * axes_flat[0][2]
        + blur_var
    )
    cov_xy = (
        axes_flat[0][0] * axes_flat[1][0]
        + axes_flat[0][1] * axes_flat[1][1]
        + axes_flat[0][2] * axes_flat[1][2]
    )
    cov_yy = (
        axes_flat[1][0] * axes_flat[1][0]
        + axes_flat[1][1] * axes_flat[1][1]
        + axes_flat[1][2] * axes_flat[1][2]
        + blur_var
    )
    determinant = cov_xx * cov_yy - cov_xy * cov_xy
    prec_xx = cov_yy / determinant
    prec_xy = -cov_xy / determinant
    prec_yy = cov_xx / determinant
    off_x = pixel_x[:, None] - mean_x[None, :]
    off_y = pixel_y[:, None] - mean_y[None, :]
    quadric = (
        prec_xx[None, :] * off_x * off_x
        + 2.0 * prec_xy[None, :] * off_x * off_y
        + prec_yy[None, :] * off_y * off_y
    )
    opacity = opacity_cap * jax.nn.sigmoid(splats[10]) * live_mask
    alpha_val = opacity[None, :] * jnp.exp(-0.5 * quadric)
    log_keep = jnp.log1p(-alpha_val)
    weights = jnp.exp(jnp.cumsum(log_keep, axis=1) - log_keep) * alpha_val
    eye_pos = [
        -(
            cam_rot[0][col_idx] * shift_vec[0]
            + cam_rot[1][col_idx] * shift_vec[1]
            + cam_rot[2][col_idx] * shift_vec[2]
        )
        for col_idx in range(3)
    ]
    view_dir = [centre[col_idx] - eye_pos[col_idx] for col_idx in range(3)]
    inverse = lax.rsqrt(
        view_dir[0] * view_dir[0] + view_dir[1] * view_dir[1] + view_dir[2] * view_dir[2]
    )
    terms = sh_terms(view_dir[0] * inverse, view_dir[1] * inverse, view_dir[2] * inverse)
    colours = jnp.stack(
        [
            sum((terms[term_idx] * splats[11 + 3 * term_idx + chan_idx] for term_idx in range(16)))
            + 0.5
            for chan_idx in range(3)
        ]
    )
    picture = jnp.einsum("pk,ck->cp", weights, colours, precision=highest)
    return 0.5 * jnp.sum((picture - goal_img) * (picture - goal_img))


def render_all(splats, live_vals, cameras, observed, tile_idx, centre_y):
    list_count = splats.shape[0]
    screens = list_count // cameras.shape[0]
    pixel_ids = jnp.arange(PIX, dtype=jnp.int32)

    def render_one(packed):
        splat_cols, live_mask, goal_img, list_idx = packed
        camera = cameras[list_idx // screens]
        number = tile_idx * screens + list_idx % screens
        pixel_x = (16 * (number % 8) + pixel_ids % 16).astype(jnp.float32) + 0.5
        pixel_y = (16 * (number // 8) + pixel_ids // 16).astype(jnp.float32) + 0.5
        return render_list(splat_cols, live_mask, camera, pixel_x, pixel_y, centre_y, goal_img)

    losses = lax.map(
        jax.checkpoint(render_one),
        (splats, live_vals, observed, jnp.arange(list_count, dtype=jnp.int32)),
    )
    return jnp.sum(losses)


def local_grad(splats, live_vals, cameras, observed, tile_idx, centre_y):

    def loss_of(inputs):
        return render_all(inputs, live_vals, cameras, observed, tile_idx, centre_y)

    loss_val, pullback = jax.vjp(loss_of, splats)
    return pullback(jnp.ones_like(loss_val))[0]


def adam_step(values, moment_one, moment_two, grads, step):
    moment_one = beta_one * moment_one + (1.0 - beta_one) * grads
    moment_two = beta_two * moment_two + (1.0 - beta_two) * grads * grads
    corr_one = 1.0 - beta_one**step
    corr_two = 1.0 - beta_two**step
    values = values - learn_rate * (moment_one / corr_one) / (
        jnp.sqrt(moment_two / corr_two) + adam_eps
    )
    return (values, moment_one, moment_two)


def on_device(
    params, moment1, moment2, tile_lists, cameras, targets, boundary_index, links, consensus, duals
):
    tile_total = lax.axis_size("tile")
    block_total = lax.axis_size("block")
    tile_idx = lax.axis_index("tile")
    block_idx = lax.axis_index("block")
    list_ids = tile_lists[0]
    list_count, klist = list_ids.shape
    per_tile = params.shape[1]
    centre_y = 8.0 * (tile_total * SCREENS // 8)
    live_mask = list_ids >= 0
    live_vals = live_mask.astype(jnp.float32)
    safe_ids = jnp.where(live_mask, list_ids, 0)
    flat_ids = safe_ids.reshape(-1)
    side_ids = boundary_index[0].reshape(-1)
    side_width = boundary_index.shape[2]
    link_vals = links.astype(jnp.float32)
    right_w = jnp.where(block_idx < block_total - 1, link_vals[block_idx], 0.0)
    left_w = jnp.where(block_idx > 0, link_vals[jnp.maximum(block_idx - 1, 0)], 0.0)
    side_w = jnp.stack([left_w, right_w])[:, None, None]
    agreed = consensus[0]
    dual_vars = duals[0]

    def gather_sides(values):
        return jnp.take(values, side_ids, axis=1).reshape(PARAMS, 2, side_width).transpose(1, 0, 2)

    values = params
    moment_one = moment1
    moment_two = moment2
    for round_idx in range(ROUNDS):
        block_vals = lax.all_gather(values, "tile", axis=1, tiled=True)
        picked = jnp.take(block_vals, flat_ids, axis=1)
        splats = picked.reshape(PARAMS, list_count, klist).transpose(1, 0, 2)
        flat_grads = (
            local_grad(splats, live_vals, cameras[0], targets[0], tile_idx, centre_y)
            .transpose(1, 0, 2)
            .reshape(PARAMS, list_count * klist)
        )
        summed = (
            jnp.zeros((PARAMS, tile_total * per_tile), jnp.float32).at[:, flat_ids].add(flat_grads)
        )
        result = lax.psum_scatter(summed, "tile", scatter_dimension=1, tiled=True)
        grads = result
        own_sides = gather_sides(values)
        prox = penalty * side_w * (own_sides - agreed + dual_vars)
        grads = grads.at[:, side_ids].add(prox.transpose(1, 0, 2).reshape(PARAMS, 2 * side_width))
        values, moment_one, moment_two = adam_step(
            values, moment_one, moment_two, grads, first_step + round_idx + 1
        )
        own_sides = gather_sides(values)
        shared = own_sides + dual_vars
        from_left = shifted(shared[1], "block", 1)
        from_right = shifted(shared[0], "block", -1)
        partner = jnp.stack([from_left, from_right])
        agreed = side_w * (shared + partner) * 0.5 + (1.0 - side_w) * own_sides
        dual_vars = dual_vars + side_w * (own_sides - agreed)
    return (values, moment_one, moment_two, agreed[None], dual_vars[None])


def solution(mesh):
    placed = (
        P(None, ("block", "tile")),
        P(None, ("block", "tile")),
        P(None, ("block", "tile")),
        P(("block", "tile"), None, None),
        P("block", None, None),
        P(("block", "tile"), None, None, None),
        P(("block", "tile"), None, None),
        P(),
        P(("block", "tile"), None, None, None),
        P(("block", "tile"), None, None, None),
    )
    return jax.shard_map(
        on_device,
        mesh=mesh,
        in_specs=placed,
        out_specs=(
            P(None, ("block", "tile")),
            P(None, ("block", "tile")),
            P(None, ("block", "tile")),
            P(("block", "tile"), None, None, None),
            P(("block", "tile"), None, None, None),
        ),
        check_vma=False,
    )
```

profile of v0, /device:TPU:198, one launch (start us, length us, event | category | flops | bytes accessed | tf_op | source)
XLA Modules:
  0.0 781.1 jit_solution(11140028492446768785)
XLA Ops:
  12.0 45.0 %all-gather.3.cloned.1.call-done = f32[59,8192]{0,1:T(8,128)} async-done(((f32[59,512]{0,1:T(8,128)}), f32[59,8192]{0,1:T(8,128)}) %all-gather.3.cloned.1.call-update) | async-done | bytes 1933328 | tf_op jit(solution)/shard_map/all_gather | solution.py:265
  56.9 7.6 gather_fusion
  65.3 233.9 %while.32 = (s32[]{:T(128)}, f32[8,59,256]{2,1,0:T(8,128)S(1)}, f32[8,59,256]{2,1,0:T(8,128)S(1)}, f32[8,256]{1,0:T(8,128)S(1)}, f32[8,3,256]{2,1,0:T(4,128)S(1)...) while((s32[]{:T(128)}, f32[8,59,256]{2,1,0:T(8,128)S(1)}, ...), condition=%wide.region_11.13_spmd.clone, body=%wide.region_0.12_spmd.clone.sunk | while | flops 31733364 | bytes 7439169 | solution.py:207
  89.5 2.3 fusion.313
  118.7 2.3 fusion.313
  148.0 2.3 fusion.313
  177.2 2.3 fusion.313
  235.7 2.3 fusion.313
  294.2 2.3 fusion.313
  300.2 14.9 %scatter_custom_fusion = f32[59,8192]{0,1:T(8,128)} fusion(s32[2048]{0:T(1024)S(1)} %bitcast.553, f32[2048,59]{1,0:T(8,128)S(1)} %copy.123, f32[]{:T(128)} %constant.845.clone.1), kind=kCustom, calls=%fused_computation.657 | custom fusion | flops 120832 | bytes 1933316 | tf_op jit(solution)/shard_map/scatter-add | solution.py:274
  318.4 61.2 %reduce-scatter.3.cloned.1.call-done = f32[59,512]{0,1:T(8,128)} async-done(((f32[59,8192]{0,1:T(8,128)}), f32[59,512]{0,1:T(8,128)}) %reduce-scatter.3.cloned.1.call-update) | async-done | bytes 120848 | tf_op jit(solution)/shard_map/reduce_scatter | solution.py:276
  379.7 3.4 scatter_fusion
  385.2 40.8 %all-gather.5.cloned.1.call-done = f32[59,8192]{1,0:T(8,128)} async-done(((f32[59,512]{1,0:T(8,128)}), f32[59,8192]{1,0:T(8,128)}) %all-gather.5.cloned.1.call-update) | async-done | bytes 1933328 | tf_op jit(solution)/shard_map/all_gather | solution.py:265
  425.9 3.8 copy.130
  429.8 7.6 gather_fusion.2
  438.2 234.5 %while.33 = (s32[]{:T(128)}, f32[8,59,256]{2,1,0:T(8,128)S(1)}, f32[8,59,256]{2,1,0:T(8,128)S(1)}, f32[8,256]{1,0:T(8,128)S(1)}, f32[8,3,256]{2,1,0:T(4,128)S(1)...) while((s32[]{:T(128)}, f32[8,59,256]{2,1,0:T(8,128)S(1)}, ...), condition=%wide.region_26.29_spmd.clone, body=%wide.region_15.28_spmd.clone.sunk | while | flops 31733364 | bytes 7439169 | solution.py:207
  462.4 2.3 fusion.329
  673.6 14.9 %scatter_custom_fusion.2 = f32[59,8192]{0,1:T(8,128)} fusion(s32[2048]{0:T(1024)S(1)} %bitcast.554, f32[2048,59]{1,0:T(8,128)S(1)} %copy.133, f32[]{:T(128)} %constant.845.clone.1), kind=kCustom, calls=%fused_computation.655 | custom fusion | flops 120832 | bytes 1933316 | tf_op jit(solution)/shard_map/scatter-add | solution.py:274
  689.7 4.8 collective-permute-start
  696.6 7.1 collective-permute-done.1
  704.0 49.5 %reduce-scatter.5.cloned.1.call-done = f32[59,512]{0,1:T(8,128)} async-done(((f32[59,8192]{0,1:T(8,128)}), f32[59,512]{0,1:T(8,128)}) %reduce-scatter.5.cloned.1.call-update) | async-done | bytes 120848 | tf_op jit(solution)/shard_map/reduce_scatter | solution.py:276
  753.5 3.4 scatter_fusion.1
  760.1 4.5 collective-permute-start.2
  766.6 7.2 collective-permute-done.3
  (1018 shorter events, 206.2 us)
Async XLA Ops:
  7.2 49.8 %all-gather.3.cloned.1.call-start = ((), (), s32[]{:S(2)}) async-start(), calls=%async_computation.2 | async-start | bytes 4456448 | tf_op jit(solution)/shard_map/all_gather | solution.py:265
  9.0 370.7 %reduce-scatter.3.cloned.1.call-start = ((), (), s32[]{:S(2)}) async-start(), calls=%async_computation.3 | async-start | bytes 4456448 | tf_op jit(solution)/shard_map/reduce_scatter | solution.py:276
  11.9 53.4 %copy-start.9 = (f32[1,2,8]{2,1,0:T(2,128)S(1)}, f32[1,2,8]{2,1,0:T(2,128)}, u32[]{:S(2)}) copy-start(f32[1,2,8]{2,1,0:T(2,128)} %param.22) | copy-start | bytes 196
  300.1 15.1 %copy-start.10 = (s32[32]{0:T(128)S(1)}, s32[32]{0:T(128)}, u32[]{:S(2)}) copy-start(s32[32]{0:T(128)} %param.25) | copy-start | bytes 388
  300.1 15.1 %copy-start.8 = (s32[1,2,128]{2,1,0:T(2,128)S(1)}, s32[1,2,128]{2,1,0:T(2,128)}, u32[]{:S(2)}) copy-start(s32[1,2,128]{2,1,0:T(2,128)} %param.24) | copy-start | bytes 3076
  300.1 15.1 %copy-start = (f32[59,512]{0,1:T(8,128)S(1)}, f32[59,512]{0,1:T(8,128)}, u32[]{:S(2)}) copy-start(f32[59,512]{0,1:T(8,128)} %copy.119) | copy-start | bytes 362500
  300.2 18.0 %copy-start.2 = (f32[1,2,59,128]{3,1,2,0:T(2,128)S(1)}, f32[1,2,59,128]{3,1,2,0:T(2,128)}, u32[]{:S(2)}) copy-start(f32[1,2,59,128]{3,1,2,0:T(2,128)} %param.27) | copy-start | bytes 181252
  300.2 18.0 %copy-start.7 = (f32[1,2,59,128]{3,1,2,0:T(2,128)S(1)}, f32[1,2,59,128]{3,1,2,0:T(2,128)}, u32[]{:S(2)}) copy-start(f32[1,2,59,128]{3,1,2,0:T(2,128)} %param.26) | copy-start | bytes 181252
  315.1 69.1 %copy-start.3 = (f32[59,512]{1,0:T(8,128)S(1)}, f32[59,512]{1,0:T(8,128)}, u32[]{:S(2)}) copy-start(f32[59,512]{1,0:T(8,128)} %param.18) | copy-start | bytes 362500
  315.1 69.1 %copy-start.4 = (f32[59,512]{1,0:T(8,128)S(1)}, f32[59,512]{1,0:T(8,128)}, u32[]{:S(2)}) copy-start(f32[59,512]{1,0:T(8,128)} %param.19) | copy-start | bytes 362500
  315.1 69.1 %copy-start.5 = (f32[59,512]{1,0:T(8,128)S(1)}, f32[59,512]{1,0:T(8,128)}, u32[]{:S(2)}) copy-start(f32[59,512]{1,0:T(8,128)} %param.20) | copy-start | bytes 362500
  315.1 110.8 %all-gather.5.cloned.1.call-start = ((), (), s32[]{:S(2)}) async-start(), calls=%async_computation.4 | async-start | bytes 2228224 | tf_op jit(solution)/shard_map/all_gather | solution.py:265
  385.0 368.5 %reduce-scatter.5.cloned.1.call-start = ((), (), s32[]{:S(2)}) async-start(), calls=%async_computation.5 | async-start | bytes 4456448 | tf_op jit(solution)/shard_map/reduce_scatter | solution.py:276
  673.6 15.0 %copy-start.1 = (f32[59,512]{1,0:T(8,128)S(1)}, f32[59,512]{1,0:T(8,128)}, u32[]{:S(2)}) copy-start(f32[59,512]{1,0:T(8,128)} %divide_subtract_fusion.1) | copy-start | bytes 362500
  689.7 6.8 collective-permute-start
  694.5 9.1 %collective-permute-start.1 = (f32[59,128]{1,0:T(8,128)S(1)}, f32[59,128]{1,0:T(8,128)S(1)}, u32[]{:S(2)}, u32[]{:S(2)}) collective-permute-start(f32[59,128]{1,0:T(8,128)S(1)} %get-tuple-element.1029), channel_id=1, source_target_pairs={{16,0},{32,16},{48,32},{64,48},{80,64},{96,80},{112,96},{128,112},... | collective-permute-start | bytes 90632 | tf_op jit(solution)/shard_map/ppermute | solution.py:44
  758.8 15.8 %copy-start.6 = (f32[59,512]{1,0:T(8,128)}, f32[59,512]{1,0:T(8,128)S(1)}, u32[]{:S(2)}) copy-start(f32[59,512]{1,0:T(8,128)S(1)} %get-tuple-element.805) | copy-start | bytes 362500
  760.1 6.5 collective-permute-start.2
  764.6 9.1 %collective-permute-start.3 = (f32[59,128]{1,0:T(8,128)S(1)}, f32[59,128]{1,0:T(8,128)S(1)}, u32[]{:S(2)}, u32[]{:S(2)}) collective-permute-start(f32[59,128]{1,0:T(8,128)S(1)} %bitcast.549), channel_id=1, source_target_pairs={{16,0},{32,16},{48,32},{64,48},{80,64},{96,80},{112,96},{128,112},... | collective-permute-start | bytes 90632 | tf_op jit(solution)/shard_map/ppermute | solution.py:44
Sparse Core Ops, SparseCore 0:
  10.1 46.7 all-gather.2
  315.3 64.3 reduce-scatter.2
  385.1 40.8 all-gather.4
  688.7 64.7 reduce-scatter.4
where the time goes:
time: 786 us; the launch traced here: 781 us
  loops' own time  268 us (34%)
  waiting for transfers between devices  211 us (27%)
  other arithmetic  192 us (24%)
  local copies, waits for them, and re-layouts  64.4 us (8%)
  matrix products  17.5 us (2%)
  between operations  15.5 us (2%)
  starting transfers between devices  13.5 us (2%)
    another operation x2, loops' own time, render_all(): lax.map(jax.checkpoint(render_one), (splats, live_vals, observed, jnp.ara...  268 us
    reduce_scatter x2, waiting for transfers between devices, on_device(): result = lax.psum_scatter(summed, 'tile', scatter_dimension=1, tiled=True)  111 us
    all_gather x2, waiting for transfers between devices, on_device(): block_vals = lax.all_gather(values, 'tile', axis=1, tiled=True)  85.7 us
    another operation x96, other arithmetic  53.3 us
    add x16, other arithmetic, render_list(): mean_x = focal_len * in_cam[0] * inv_depth + 64.0  30.8 us
    scatter-add x2, other arithmetic, on_device(): jnp.zeros((PARAMS, tile_total * per_tile), jnp.float32).at[:, flat_ids]  29.8 us
    add x16, other arithmetic, render_list(): mean_y = focal_len * in_cam[1] * inv_depth + centre_y  20.5 us
    dot_general x48, matrix products, render_list(): picture = jnp.einsum('pk,ck->cp', weights, colours, precision=highest)  17.5 us
  transfers between devices with their start and end apart: 8, of which 6 were waited for; matrix products, arithmetic and copies ran while one was open for 1% of the time, Pallas kernels for 0%

commit v1 on v0

v1 whole, which is shorter than its diff:
```python
import functools
import jax
import jax.numpy as jnp
from jax import lax
from jax.experimental import pallas as pl
from jax.experimental.pallas import tpu as pltpu
from jax.sharding import PartitionSpec as P

PARAMS = 59
SCREENS = 4
ROUNDS = 2
LISTS = 8
CAP = 16
SLOTS = 256
TILES = 16
SPL = 512
NB = 128
ROWS = 16
FEATS = 9
WIDE = 72
TOGETHER = 2
GRANT = 10 << 20

sh_zero = 0.28209479177387814
sh_one = 0.4886025119029199
sh_two = (
    1.0925484305920792,
    -1.0925484305920792,
    0.31539156525252005,
    -1.0925484305920792,
    0.5462742152960396,
)
sh_three = (
    -0.5900435899266435,
    2.890611442640554,
    -0.4570457994644658,
    0.3731763325901154,
    -0.4570457994644658,
    1.445305721320277,
    -0.5900435899266435,
)
beta_one = 0.9
beta_two = 0.999
learn_rate = 0.01
adam_eps = 1e-08
penalty = 2.0
first_step = 100
blur_var = 0.3
opacity_cap = 0.99
log2e = 1.4426950408889634

f32 = jnp.float32
bf16 = jnp.bfloat16
i32 = jnp.int32
VMEM = pltpu.VMEM
ANY_VMEM = pl.BlockSpec(memory_space=pltpu.VMEM)
ANY_SMEM = pl.BlockSpec(memory_space=pltpu.SMEM)


def iota(shape, axis):
    return lax.broadcasted_iota(i32, shape, axis)


def dot(a, b):
    return lax.dot_general(a, b, (((1,), (0,)), ((), ())), preferred_element_type=f32)


def dot_t(a, b):
    return lax.dot_general(a, b, (((1,), (1,)), ((), ())), preferred_element_type=f32)


def split(value):
    high = value.astype(bf16)
    return high, (value - high.astype(f32)).astype(bf16)


def lane_gather(value, index):
    return jnp.take_along_axis(value, index, axis=1, mode="promise_in_bounds")


def rotation(quat_w, quat_x, quat_y, quat_z):
    inverse = lax.rsqrt(quat_w * quat_w + quat_x * quat_x + quat_y * quat_y + quat_z * quat_z)
    unit_w = quat_w * inverse
    unit_x = quat_x * inverse
    unit_y = quat_y * inverse
    unit_z = quat_z * inverse
    return (
        (
            1.0 - 2.0 * (unit_y * unit_y + unit_z * unit_z),
            2.0 * (unit_x * unit_y - unit_w * unit_z),
            2.0 * (unit_x * unit_z + unit_w * unit_y),
        ),
        (
            2.0 * (unit_x * unit_y + unit_w * unit_z),
            1.0 - 2.0 * (unit_x * unit_x + unit_z * unit_z),
            2.0 * (unit_y * unit_z - unit_w * unit_x),
        ),
        (
            2.0 * (unit_x * unit_z - unit_w * unit_y),
            2.0 * (unit_y * unit_z + unit_w * unit_x),
            1.0 - 2.0 * (unit_x * unit_x + unit_y * unit_y),
        ),
    )


def sh_terms(dir_x, dir_y, dir_z):
    sq_x = dir_x * dir_x
    sq_y = dir_y * dir_y
    sq_z = dir_z * dir_z
    return (
        -sh_one * dir_y,
        sh_one * dir_z,
        -sh_one * dir_x,
        sh_two[0] * dir_x * dir_y,
        sh_two[1] * dir_y * dir_z,
        sh_two[2] * (2.0 * sq_z - sq_x - sq_y),
        sh_two[3] * dir_x * dir_z,
        sh_two[4] * (sq_x - sq_y),
        sh_three[0] * dir_y * (3.0 * sq_x - sq_y),
        sh_three[1] * dir_x * dir_y * dir_z,
        sh_three[2] * dir_y * (4.0 * sq_z - sq_x - sq_y),
        sh_three[3] * dir_z * (2.0 * sq_z - 3.0 * sq_x - 3.0 * sq_y),
        sh_three[4] * dir_x * (4.0 * sq_z - sq_x - sq_y),
        sh_three[5] * dir_z * (sq_x - sq_y),
        sh_three[6] * dir_x * (sq_x - 3.0 * sq_y),
    )


def camera_of(cam_ref):
    first = iota((8, 128), 0) < 4
    vals = [jnp.where(first, cam_ref[0, 0, i], cam_ref[0, 1, i]) for i in range(8)]
    rot = rotation(vals[0], vals[1], vals[2], vals[3])
    shift = vals[4:7]
    eye = [-(rot[0][c] * shift[0] + rot[1][c] * shift[1] + rot[2][c] * shift[2]) for c in range(3)]
    return rot, shift, vals[7], eye


def geometry(centre, log_scales, quat, cam):
    cam_rot, shift, focal, _ = cam
    in_cam = [
        cam_rot[r][0] * centre[0] + cam_rot[r][1] * centre[1] + cam_rot[r][2] * centre[2] + shift[r]
        for r in range(3)
    ]
    inv_depth = 1.0 / in_cam[2]
    scaled = focal * inv_depth
    ratio_x = in_cam[0] * inv_depth
    ratio_y = in_cam[1] * inv_depth
    mean_x = focal * ratio_x
    mean_y = focal * ratio_y
    screen_map = [
        [scaled * (cam_rot[0][c] - ratio_x * cam_rot[2][c]) for c in range(3)],
        [scaled * (cam_rot[1][c] - ratio_y * cam_rot[2][c]) for c in range(3)],
    ]
    local_rot = rotation(*quat)
    scales = [jnp.exp(s) for s in log_scales]
    axes = [
        [
            (
                screen_map[r][0] * local_rot[0][c]
                + screen_map[r][1] * local_rot[1][c]
                + screen_map[r][2] * local_rot[2][c]
            )
            * scales[c]
            for c in range(3)
        ]
        for r in range(2)
    ]
    cov_xx = axes[0][0] * axes[0][0] + axes[0][1] * axes[0][1] + axes[0][2] * axes[0][2] + blur_var
    cov_xy = axes[0][0] * axes[1][0] + axes[0][1] * axes[1][1] + axes[0][2] * axes[1][2]
    cov_yy = axes[1][0] * axes[1][0] + axes[1][1] * axes[1][1] + axes[1][2] * axes[1][2] + blur_var
    return mean_x, mean_y, cov_xx, cov_xy, cov_yy


def colours_of(centre, coeffs, cam):
    eye = cam[3]
    view = [centre[c] - eye[c] for c in range(3)]
    inverse = lax.rsqrt(view[0] * view[0] + view[1] * view[1] + view[2] * view[2])
    terms = sh_terms(view[0] * inverse, view[1] * inverse, view[2] * inverse)
    out = []
    for ch in range(3):
        total = sh_zero * coeffs[ch] + 0.5
        for q in range(15):
            total = total + terms[q] * coeffs[3 * (q + 1) + ch]
        out.append(total)
    return out


def precision_of(cov_xx, cov_xy, cov_yy):
    inverse = 1.0 / (cov_xx * cov_yy - cov_xy * cov_xy)
    return cov_yy * inverse, -cov_xy * inverse, cov_xx * inverse


def spread(x_ref, wide):
    for a in range(0, PARAMS, 8):
        n = min(8, PARAMS - a)
        for k in range(4):
            piece = x_ref[a : a + n, 128 * k : 128 * (k + 1)]
            for v in range(2):
                wide[pl.ds(8 * a + 4 * v + k, n, stride=8), :] = piece


def wide_row(wide, i):
    return wide[8 * i : 8 * i + 8, :]


def make_features(wide, cam, centre_y, feat):
    centre = [wide_row(wide, i) for i in range(3)]
    geo = geometry(
        centre, [wide_row(wide, 3 + i) for i in range(3)], [wide_row(wide, 6 + i) for i in range(4)], cam
    )
    prec = precision_of(geo[2], geo[3], geo[4])
    cols = colours_of(centre, [wide_row(wide, 11 + i) for i in range(48)], cam)
    opac = opacity_cap * jax.nn.sigmoid(wide_row(wide, 10))
    values = (*cols, geo[0] + 64.0, geo[1] + centre_y, *prec, opac)
    for f in range(FEATS):
        feat[8 * f : 8 * f + 8, :] = values[f]


def pick_features(sources, opac, index_row):
    row = iota((8, 128), 0)
    first = iota((8, 128), 1) < 64
    index = jnp.broadcast_to(jnp.maximum(index_row, 0), (8, 128))
    low = index & 127
    part = index >> 7
    both = []
    for v in range(2):
        got = [lane_gather(sources[v][k], low) for k in range(4)]
        both.append(
            jnp.where(part < 2, jnp.where(part == 0, got[0], got[1]), jnp.where(part == 2, got[2], got[3]))
        )
    last = jnp.where(row == jnp.where(first, 0, 4) + part, lane_gather(opac, low), 0.0)
    return jnp.where(first, both[0], both[1]), jnp.sum(last, axis=0, keepdims=True)


def sources_of(load):
    return [[load(pl.ds(4 * v + k, 8, stride=8)) for k in range(4)] for v in range(2)]


def lists_kernel(lists_ref, bidx_ref, before_ref, live_ref, req_ref, inv_ref):
    sub = iota((SLOTS, SLOTS), 0)
    lane = iota((SLOTS, SLOTS), 1)
    upto = jnp.where(sub <= lane, 1.0, 0.0).astype(bf16)
    number = (iota((SLOTS, 128), 0) + 1).astype(f32).astype(bf16)
    slot = iota((1, SLOTS), 1)
    row8 = iota((8, SLOTS), 0)
    owners = iota((TILES, SLOTS), 0)
    row = iota((8, 128), 0)
    col = iota((8, 128), 1)
    pick = row * CAP + (col & (CAP - 1))
    acc = [jnp.full((8, 128), -1, i32) for _ in range(2)]
    for l in range(LISTS):
        ids = lists_ref[0, l : l + 1, :]
        live = ids >= 0
        owner = jnp.where(live, ids >> 9, -1)
        local = ids & (SPL - 1)
        mine = owner == owners
        counts = dot(jnp.where(mine, 1.0, 0.0).astype(bf16), upto)
        rank = jnp.sum(jnp.where(mine, counts, 0.0), axis=0, keepdims=True).astype(i32) - 1
        place = jnp.where(live, owner * CAP + rank, -1)
        chosen = jnp.where(place == sub, 1.0, 0.0).astype(bf16)
        rows = jnp.where(
            row8 == 0, slot + 1, jnp.where(row8 == 1, local & 255, jnp.where(row8 == 2, local >> 8, 0))
        )
        found = dot_t(rows.astype(f32).astype(bf16), chosen)
        order = found[0:1, :]
        column = dot(chosen, number)
        before_ref[l] = jnp.where(jnp.concatenate([column, column], axis=1) < order, 1.0, 0.0).astype(bf16)
        held = order > 0.5
        live_ref[l : l + 1, :] = jnp.where(held, 1.0, 0.0)
        wanted = jnp.where(held, found[1:2, :] + 256.0 * found[2:3, :], -1.0).astype(i32)
        for h in range(2):
            half = jnp.broadcast_to(wanted[:, 128 * h : 128 * (h + 1)], (8, 128))
            acc[h] = jnp.where((col >> 4) == l, lane_gather(half, pick), acc[h])
    for o in range(TILES):
        req_ref[o] = acc[o // 8][o % 8 : o % 8 + 1, :]
    total = jnp.zeros((8, SPL), f32)
    sub_n = iota((SPL, NB), 0)
    for e in range(2):
        hit = jnp.where(bidx_ref[0, e : e + 1, :] == sub_n, 1.0, 0.0).astype(bf16)
        total = total + dot_t((col + (NB * e + 1)).astype(f32).astype(bf16), hit)
    inv_ref[...] = total.astype(i32) - 1


def features_kernel(centre_y, x_ref, cam_ref, feat_ref, wide):
    spread(x_ref, wide)
    make_features(wide, camera_of(cam_ref), centre_y, feat_ref)


def render_kernel(
    first_round,
    tile_ref,
    msg_in,
    before_ref,
    live_ref,
    goal_ref,
    *rest,
):
    if first_round:
        req_ref, out_ref, msg_ref = rest[0], rest[1], rest[-1]
        rest = rest[2:-1]
        for o in range(TILES):
            main, last = pick_features(
                sources_of(lambda rows: msg_in[o, rows, :]), msg_in[o, 64:72, :], req_ref[o]
            )
            msg_ref[o, 0:8, :] = main
            msg_ref[o, 8:9, :] = last
            out_ref[o, 9:10, :] = req_ref[o].astype(f32)
    else:
        msg_ref, out_ref = msg_in, rest[0]
        rest = rest[1:]
    feat, grad, grad8, goal8, alpha, lk_h, lk_l, wgt, wgt_h, wgt_l, u_f, u_h, u_l = rest
    row = iota((8, 128), 0)
    col = iota((8, 128), 1)
    block = col >> 4
    inner = col & (CAP - 1)
    for h in range(2):
        whole = [msg_ref[8 * h + o, 0:8, :] for o in range(8)]
        ninth = jnp.concatenate([msg_ref[8 * h + o, 8:9, :] for o in range(8)], axis=0)
        for l in range(LISTS):
            got = whole[l]
            for o in range(8):
                if o != l:
                    got = jnp.where(block == o, pltpu.roll(whole[o], (o - l) * CAP % 128, 1), got)
            feat[l, 0:8, 128 * h : 128 * (h + 1)] = got
            last = jnp.where(row == block, lane_gather(ninth, inner + CAP * l), 0.0)
            feat[l, 8:9, 128 * h : 128 * (h + 1)] = jnp.sum(last, axis=0, keepdims=True)
    goal8[...] = jnp.zeros_like(goal8)
    tile = tile_ref[0]
    sub16 = iota((16, SLOTS), 0).astype(f32)
    row8 = iota((8, SLOTS), 0)
    half = -0.5 * log2e
    group = range(TOGETHER)
    down = functools.partial(jnp.sum, axis=0, keepdims=True)

    def some_lists(step, carry):
        lists = [step * TOGETHER + i for i in group]
        f8, opac, off_x, start_y, mean_y, quad_a, quad_b, prec_y = ([None] * TOGETHER for _ in range(8))
        for i, l in enumerate(lists):
            number = tile * SCREENS + lax.rem(l, SCREENS)
            start_x = (16 * lax.rem(number, 8)).astype(f32) + 0.5
            start_y[i] = (16 * lax.div(number, 8)).astype(f32) + 0.5
            f8[i] = feat[l, 0:8, :]
            opac[i] = feat[l, 8:9, :] * live_ref[pl.ds(l, 1), :]
            off_x[i] = (sub16 + start_x) - f8[i][3:4, :]
            quad_a[i] = (half * f8[i][5:6, :]) * off_x[i] * off_x[i]
            quad_b[i] = (2.0 * half * f8[i][6:7, :]) * off_x[i]
            prec_y[i] = half * f8[i][7:8, :]
            mean_y[i] = f8[i][4:5, :]
        for y in range(16):
            rows = slice(16 * y, 16 * y + 16)
            for i in group:
                off_y = (start_y[i] + float(y)) - mean_y[i]
                quad = quad_a[i] + (off_y * quad_b[i] + prec_y[i] * off_y * off_y)
                a = opac[i] * jnp.exp2(quad)
                high, low = split(jnp.log(1.0 - a))
                alpha[i, rows, :] = a
                lk_h[i, rows, :] = high
                lk_l[i, rows, :] = low
        before = [before_ref[l] for l in lists]
        for c in range(4):
            rows = slice(64 * c, 64 * c + 64)
            for i in group:
                total = dot(lk_h[i, rows, :], before[i]) + dot(lk_l[i, rows, :], before[i])
                w = jnp.exp2(total * log2e) * alpha[i, rows, :]
                high, low = split(w)
                wgt[i, rows, :] = w
                wgt_h[i, rows, :] = high
                wgt_l[i, rows, :] = low
        left, right, d_h, d_l = ([None] * TOGETHER for _ in range(4))
        for i, l in enumerate(lists):
            c_h, c_l = split(f8[i])
            image = dot_t(c_h, wgt_h[i]) + (dot_t(c_h, wgt_l[i]) + dot_t(c_l, wgt_h[i]))
            goal8[i, 0:3, :] = goal_ref[0, l]
            diff = jnp.where(row8 < 3, image - goal8[i], 0.0)
            d_h[i], d_l[i] = split(diff)
            d_hf = d_h[i].astype(f32)
            d_lf = d_l[i].astype(f32)
            c_hf = c_h.astype(f32)
            c_lf = c_l.astype(f32)
            left[i] = jnp.transpose(jnp.concatenate([d_hf, d_hf, d_lf, d_lf], axis=0)).astype(bf16)
            right[i] = jnp.concatenate([c_hf, c_lf, c_hf, c_lf], axis=0).astype(bf16)
        for c in range(4):
            rows = slice(64 * c, 64 * c + 64)
            for i in group:
                u = wgt[i, rows, :] * dot(left[i][rows, :], right[i])
                high, low = split(u)
                u_f[i, rows, :] = u
                u_h[i, rows, :] = high
                u_l[i, rows, :] = low
        sums = [[jnp.zeros((16, SLOTS), f32) for _ in range(3)] for _ in group]
        for c in range(4):
            rows = slice(64 * c, 64 * c + 64)
            for i in group:
                later = dot_t(u_h[i, rows, :], before[i]) + dot_t(u_l[i, rows, :], before[i])
                a = alpha[i, rows, :]
                slope = u_f[i, rows, :] - later * (a / (1.0 - a))
                for y in range(4):
                    off_y = (start_y[i] + float(4 * c + y)) - mean_y[i]
                    part = slope[16 * y : 16 * y + 16, :]
                    moved = off_y * part
                    sums[i][0] = sums[i][0] + part
                    sums[i][1] = sums[i][1] + moved
                    sums[i][2] = sums[i][2] + off_y * moved
        for i, l in enumerate(lists):
            colour = dot(d_h[i], wgt_h[i]) + (dot(d_h[i], wgt_l[i]) + dot(d_l[i], wgt_h[i]))
            by_x = sums[i][0] * off_x[i]
            moments = (
                down(sums[i][0]),
                down(by_x),
                down(sums[i][1]),
                down(by_x * off_x[i]),
                down(sums[i][1] * off_x[i]),
            )
            for j in range(5):
                colour = jnp.where(row8 == 3 + j, moments[j], colour)
            grad[l] = colour
            grad8[pl.ds(l, 1), :] = down(sums[i][2])
        return carry

    lax.fori_loop(0, LISTS // TOGETHER, some_lists, 0)
    for h in range(2):
        lanes = slice(128 * h, 128 * (h + 1))
        whole = [grad[l, :, lanes] for l in range(LISTS)]
        ninth = grad8[:, lanes]
        for o in range(8):
            got = whole[o]
            for l in range(LISTS):
                if l != o:
                    got = jnp.where(block == l, pltpu.roll(whole[l], (l - o) * CAP % 128, 1), got)
            out_ref[8 * h + o, 0:8, :] = got
            last = jnp.where(row == block, lane_gather(ninth, inner + CAP * o), 0.0)
            out_ref[8 * h + o, 8:9, :] = jnp.sum(last, axis=0, keepdims=True)


def side_columns(x_ref, bidx_ref, a, e):
    index = jnp.broadcast_to(bidx_ref[0, e : e + 1, :], (8, NB))
    low = index & 127
    part = index >> 7
    got = [lane_gather(x_ref[a : a + 8, 128 * k : 128 * (k + 1)], low) for k in range(4)]
    return jnp.where(
        part < 2, jnp.where(part == 0, got[0], got[1]), jnp.where(part == 2, got[2], got[3])
    )


def update_kernel(
    step,
    last_round,
    centre_y,
    w_ref,
    cam_ref,
    gmsg_ref,
    *rest,
):
    if last_round:
        req_ref, *rest = rest
    (x_ref, m_ref, v_ref, bidx_ref, inv_ref, z_ref, u_ref), rest = rest[:7], rest[7:]
    (xo_ref, mo_ref, vo_ref, side_ref, sh0_ref, sh1_ref), rest = rest[:6], rest[6:]
    if last_round:
        wide, gin, gwide, terms, hits, prox, pad, grad = rest
    else:
        msg_ref, req_out, wide, feat, gin, gwide, terms, hits, prox, pad, grad = rest
    first = iota((ROWS, 128), 1) < 64
    sub_n = iota((SPL, 128), 0)
    for t in range(TILES):
        lanes = slice(128 * t, 128 * (t + 1))
        high, low = split(gmsg_ref[t])
        zero = jnp.zeros_like(high)
        terms[0:16, lanes] = jnp.where(first, high, zero)
        terms[16:32, lanes] = jnp.where(first, zero, high)
        terms[32:48, lanes] = jnp.where(first, low, zero)
        terms[48:64, lanes] = jnp.where(first, zero, low)
        if last_round:
            wanted = req_ref[t]
        else:
            wanted = gmsg_ref[t, 9:10, :].astype(i32)
            req_out[t] = wanted
        hits[:, lanes] = jnp.where(wanted == sub_n, 1.0, 0.0).astype(bf16)
    found = dot_t(terms[...], hits[...])
    total = found[0:32, :] + found[32:64, :]
    for v in range(2):
        for k in range(4):
            lanes = slice(128 * k, 128 * (k + 1))
            gin[pl.ds(4 * v + k, 8, stride=8), :] = total[16 * v : 16 * v + 8, lanes]
            gin[64 + 4 * v + k : 65 + 4 * v + k, :] = total[16 * v + 8 : 16 * v + 9, lanes]
    got = [gin[8 * f : 8 * f + 8, :] for f in range(FEATS)]

    pad[0:PARAMS, :] = x_ref[...]
    spread(x_ref, wide)
    cam = camera_of(cam_ref)
    centre = [wide_row(wide, i) for i in range(3)]
    log_scales = [wide_row(wide, 3 + i) for i in range(3)]
    quat = [wide_row(wide, 6 + i) for i in range(4)]
    coeffs = [wide_row(wide, 11 + i) for i in range(48)]
    geo, geo_back = jax.vjp(lambda a, b, c: geometry(a, b, c, cam), centre, log_scales, quat)
    p_xx, p_xy, p_yy = precision_of(geo[2], geo[3], geo[4])
    h_sum, m_x, m_y, m_xx, m_xy, m_yy = got[3:9]
    a_xx = p_xx * m_xx + p_xy * m_xy
    a_xy = p_xx * m_xy + p_xy * m_yy
    a_yx = p_xy * m_xx + p_yy * m_xy
    a_yy = p_xy * m_xy + p_yy * m_yy
    geo_grad = (
        p_xx * m_x + p_xy * m_y,
        p_xy * m_x + p_yy * m_y,
        0.5 * (a_xx * p_xx + a_xy * p_xy),
        a_xx * p_xy + a_xy * p_yy,
        0.5 * (a_yx * p_xy + a_yy * p_yy),
    )
    g_centre, g_scales, g_quat = geo_back(geo_grad)
    _, col_back = jax.vjp(lambda a, b: colours_of(a, b, cam), centre, coeffs)
    g_centre2, g_coeffs = col_back(list(got[0:3]))
    g_opac = h_sum * (1.0 - jax.nn.sigmoid(wide_row(wide, 10)))
    grads = (
        [g_centre[i] + g_centre2[i] for i in range(3)] + list(g_scales) + list(g_quat) + [g_opac] + list(g_coeffs)
    )
    for i in range(PARAMS):
        gwide[8 * i : 8 * i + 8, :] = grads[i]

    for a in range(0, PARAMS, 8):
        n = min(8, PARAMS - a)
        for e in range(2):
            mine = side_columns(pad, bidx_ref, a, e)[0:n]
            prox[a : a + n, NB * e : NB * (e + 1)] = (penalty * w_ref[e]) * (
                mine - z_ref[0, e, a : a + n, :] + u_ref[0, e, a : a + n, :]
            )
        for k in range(4):
            lanes = slice(128 * k, 128 * (k + 1))
            inverse = inv_ref[:, lanes]
            low = inverse & 127
            add = jnp.where(
                inverse < 128,
                lane_gather(prox[a : a + 8, 0:128], low),
                lane_gather(prox[a : a + 8, 128:256], low),
            )
            grad[a : a + 8, lanes] = (
                gwide[pl.ds(8 * a + k, 8, stride=8), :]
                + gwide[pl.ds(8 * a + 4 + k, 8, stride=8), :]
                + jnp.where(inverse >= 0, add, 0.0)
            )
    g = grad[0:PARAMS, :]
    m = beta_one * m_ref[...] + (1.0 - beta_one) * g
    v = beta_two * v_ref[...] + (1.0 - beta_two) * g * g
    corr_one = 1.0 - beta_one**step
    corr_two = 1.0 - beta_two**step
    x = x_ref[...] - (learn_rate / corr_one) * m / (jnp.sqrt(v * (1.0 / corr_two)) + adam_eps)
    mo_ref[...] = m
    vo_ref[...] = v
    xo_ref[...] = x
    pad[0:PARAMS, :] = x
    for a in range(0, PARAMS, 8):
        n = min(8, PARAMS - a)
        for e in range(2):
            mine = side_columns(pad, bidx_ref, a, e)[0:n]
            side_ref[e, a : a + n, :] = mine
            (sh0_ref, sh1_ref)[e][a : a + n, :] = mine + u_ref[0, e, a : a + n, :]
    if not last_round:
        spread(pad, wide)
        make_features(wide, cam, centre_y, feat)
        sources = sources_of(lambda rows: feat[rows, :])
        opac = feat[64:72, :]
        for t in range(TILES):
            main, last = pick_features(sources, opac, gmsg_ref[t, 9:10, :].astype(i32))
            msg_ref[t, 0:8, :] = main
            msg_ref[t, 8:9, :] = last


def consensus_kernel(w_ref, side_ref, u_ref, left_ref, right_ref, zo_ref, uo_ref):
    for e in range(2):
        w = w_ref[e]
        own = side_ref[e]
        dual = u_ref[0, e]
        agreed = w * (own + dual + (left_ref, right_ref)[e][...]) * 0.5 + (1.0 - w) * own
        zo_ref[:, e, :] = agreed
        uo_ref[:, e, :] = dual + w * (own - agreed)


def shape(dims, kind=f32):
    return jax.ShapeDtypeStruct(dims, kind)


def on_device(
    params, moment1, moment2, tile_lists, cameras, targets, boundary_index, links, consensus, duals
):
    block_total = lax.axis_size("block")
    tile_idx = lax.axis_index("tile")
    block_idx = lax.axis_index("block")
    centre_y = 8.0 * (TILES * SCREENS // 8)
    link_vals = links.astype(f32)
    right_w = jnp.where(block_idx < block_total - 1, link_vals[block_idx], 0.0)
    left_w = jnp.where(block_idx > 0, link_vals[jnp.maximum(block_idx - 1, 0)], 0.0)
    side_w = jnp.stack([left_w, right_w])
    tile_num = tile_idx.astype(i32).reshape(1)

    def call(kernel, name, outs, ins, scratch=()):
        return pl.pallas_call(
            kernel,
            out_shape=outs,
            in_specs=ins,
            out_specs=jax.tree.map(lambda _: ANY_VMEM, outs),
            scratch_shapes=list(scratch),
            compiler_params=pltpu.CompilerParams(vmem_limit_bytes=GRANT),
            name=name,
        )

    wide_scratch = VMEM((512, 128), f32)
    features = call(
        functools.partial(features_kernel, centre_y),
        "features",
        shape((WIDE, 128)),
        [ANY_VMEM, ANY_SMEM],
        [wide_scratch],
    )(params, cameras)
    message = lax.all_gather(features, "tile")
    before, live, wanted, inverse = call(
        lists_kernel,
        "lists",
        (
            shape((LISTS, SLOTS, SLOTS), bf16),
            shape((LISTS, SLOTS)),
            shape((TILES, 1, 128), i32),
            shape((8, SPL), i32),
        ),
        [ANY_VMEM] * 2,
    )(tile_lists, boundary_index)

    def exchange(value):
        return lax.all_to_all(value, "tile", 0, 0, tiled=True)

    def render(first_round):
        scratch = [
            VMEM((LISTS, 16, SLOTS), f32),
            VMEM((LISTS, 8, SLOTS), f32),
            VMEM((LISTS, SLOTS), f32),
            VMEM((TOGETHER, 8, SLOTS), f32),
        ]
        for kind in (f32, bf16, bf16, f32, bf16, bf16, f32, bf16, bf16):
            scratch.append(VMEM((TOGETHER, SLOTS, SLOTS), kind))
        if first_round:
            scratch.append(VMEM((TILES, ROWS, 128), f32))
        return call(
            functools.partial(render_kernel, first_round),
            "render",
            shape((TILES, ROWS, 128)),
            [ANY_SMEM] + [ANY_VMEM] * (5 if first_round else 4),
            scratch,
        )

    def shifted(x, by):
        pairs = [(i, i + by) for i in range(block_total) if 0 <= i + by < block_total]
        return lax.ppermute(x, "block", pairs)

    values, moment_one, moment_two = params, moment1, moment2
    agreed, dual_vars = consensus, duals
    requests = None
    for round_idx in range(ROUNDS):
        last_round = round_idx == ROUNDS - 1
        first_round = round_idx == 0
        if first_round:
            sent = render(True)(tile_num, message, before, live, targets, wanted)
        else:
            sent = render(False)(tile_num, exchange(message), before, live, targets)
        back = exchange(sent)
        outs = [shape((PARAMS, SPL))] * 3 + [shape((2, PARAMS, NB))] + [shape((PARAMS, NB))] * 2
        scratch = [wide_scratch]
        if not last_round:
            outs += [shape((TILES, ROWS, 128)), shape((TILES, 1, 128), i32)]
            scratch += [VMEM((WIDE, 128), f32)]
        scratch += [
            VMEM((WIDE, 128), f32),
            VMEM((512, 128), f32),
            VMEM((64, TILES * 128), bf16),
            VMEM((SPL, TILES * 128), bf16),
            VMEM((64, 2 * NB), f32),
            VMEM((64, SPL), f32),
            VMEM((64, SPL), f32),
        ]
        known = (requests,) if last_round else ()
        outs = call(
            functools.partial(update_kernel, first_step + round_idx + 1, last_round, centre_y),
            "update",
            tuple(outs),
            [ANY_SMEM, ANY_SMEM] + [ANY_VMEM] * (8 + len(known)),
            scratch,
        )(
            side_w,
            cameras,
            back,
            *known,
            values,
            moment_one,
            moment_two,
            boundary_index,
            inverse,
            agreed,
            dual_vars,
        )
        values, moment_one, moment_two, own_sides, shared0, shared1 = outs[:6]
        from_left = shifted(shared1, 1)
        from_right = shifted(shared0, -1)
        if not last_round:
            message, requests = outs[6:]
            partner = jnp.stack([from_left, from_right])[None]
            own_sides = own_sides[None]
            wide_w = side_w[None, :, None, None]
            agreed = wide_w * (own_sides + dual_vars + partner) * 0.5 + (1.0 - wide_w) * own_sides
            dual_vars = dual_vars + wide_w * (own_sides - agreed)
        else:
            sides = (shape((PARAMS, 2, NB)),) * 2
            sides = call(consensus_kernel, "consensus", sides, [ANY_SMEM] + [ANY_VMEM] * 4)(
                side_w, own_sides, dual_vars, from_left, from_right
            )
            agreed, dual_vars = (jnp.transpose(side, (1, 0, 2))[None] for side in sides)
    return (values, moment_one, moment_two, agreed, dual_vars)


def solution(mesh):
    both = ("block", "tile")
    placed = (
        P(None, both),
        P(None, both),
        P(None, both),
        P(both, None, None),
        P("block", None, None),
        P(both, None, None, None),
        P(both, None, None),
        P(),
        P(both, None, None, None),
        P(both, None, None, None),
    )
    return jax.shard_map(
        on_device,
        mesh=mesh,
        in_specs=placed,
        out_specs=(
            P(None, both),
            P(None, both),
            P(None, both),
            P(both, None, None, None),
            P(both, None, None, None),
        ),
        check_vma=False,
    )
```

time: 786 us -> 105 us (0.13)
  loops' own time: 268 us -> 0 us
  other arithmetic: 192 us -> 0.17 us
  waiting for transfers between devices: 211 us -> 23 us
  local copies, waits for them, and re-layouts: 64.4 us -> 2.95 us
  Pallas kernels: 0 us -> 26.2 us
  blocking collectives: 0 us -> 19.2 us
  matrix products: 17.5 us -> 0 us
  starting transfers between devices: 13.5 us -> 30.4 us
  between operations: 15.5 us -> 2.12 us
    another operation x2 -> x0, loops' own time: 268 us -> none  [render_all(): lax.map(jax.checkpoint(render_one), (splats, live_vals, observed, jnp.ara...]
    reduce_scatter x2 -> x0, waiting for transfers between devices: 111 us -> none  [on_device(): result = lax.psum_scatter(summed, 'tile', scatter_dimension=1, tiled=True)]
    all_gather x2 -> x0, waiting for transfers between devices: 85.7 us -> none  [on_device(): block_vals = lax.all_gather(values, 'tile', axis=1, tiled=True)]
    add x98 -> x1, other arithmetic: 53.8 us -> 0.09 us  [on_device(): dual_vars = dual_vars + wide_w * (own_sides - agreed)]
    another operation x96 -> x0, other arithmetic: 53.3 us -> none
    scatter-add x4 -> x0, other arithmetic: 36.7 us -> none  [the longest x2 29.8 us: on_device(): jnp.zeros((PARAMS, tile_total * per_tile), jnp.float32).at[:, flat_ids]]
    pallas_call x0 -> x7, Pallas kernels: none -> 26.2 us  [the longest x1 8.48 us: on_device(): sent = render(True)(tile_num, message, before, live, targets, wanted)]
    all_gather x0 -> x1, blocking collectives: none -> 19.2 us  [on_device(): message = lax.all_gather(features, 'tile')]
  transfers between devices with their start and end apart: 8 -> 7, of which waited for: 6 -> 4; matrix products, arithmetic and copies ran while one was open for 1% -> 1% of each run, Pallas kernels for 0% -> 8%
where the time goes in v1:
time: 105 us; the launch traced here: 104 us
  starting transfers between devices  30.4 us (29%)
  Pallas kernels  26.2 us (25%)
  waiting for transfers between devices  23 us (22%)
  blocking collectives  19.2 us (18%)
  local copies, waits for them, and re-layouts  2.95 us (3%)
  between operations  2.12 us (2%)
    all_gather x1, blocking collectives, on_device(): message = lax.all_gather(features, 'tile')  19.2 us
    ppermute x4, starting transfers between devices, shifted(): return lax.ppermute(x, 'block', pairs)  16.5 us
    all_to_all x3, waiting for transfers between devices, exchange(): return lax.all_to_all(value, 'tile', 0, 0, tiled=True)  15.8 us
    all_to_all x3, starting transfers between devices, exchange(): return lax.all_to_all(value, 'tile', 0, 0, tiled=True)  13.9 us
    pallas_call x1, Pallas kernels, on_device(): sent = render(True)(tile_num, message, before, live, targets, wanted)  8.48 us
    pallas_call x1, Pallas kernels, on_device(): sent = render(False)(tile_num, exchange(message), before, live, targets)  8.27 us
    ppermute x4, waiting for transfers between devices, shifted(): return lax.ppermute(x, 'block', pairs)  7.2 us
    pallas_call x2, Pallas kernels, on_device(): call(functools.partial(update_kernel, first_step + round_idx + 1, last_ro...  5.46 us
  transfers between devices with their start and end apart: 7, of which 4 were waited for; matrix products, arithmetic and copies ran while one was open for 1% of the time, Pallas kernels for 8%

profile of v1, /device:TPU:198, one launch (start us, length us, event | category | flops | bytes accessed | tf_op | source)
XLA Modules:
  0.0 104.1 jit_solution(2253132553262519071)
XLA Ops:
  0.6 0.8 copy.15.goal_ref
  1.4 0.9 copy-done
  2.3 0.6 features.1
  3.0 19.2 %all-gather = f32[1152,128]{1,0:T(8,128)S(1)} all-gather(f32[72,128]{1,0:T(8,128)S(1)} %features.1), channel_id=2, replica_groups=mesh['block'=32,'tile'=16] {'tile'}, dimensions={0}, use_global_device_ids=true | all-gather | bytes 626688 | tf_op jit(solution)/shard_map/all_gather | solution.py:612
  22.2 2.1 %lists.1 = (bf16[8,256,256]{2,1,0:T(8,128)(2,1)S(1)}, f32[8,256]{1,0:T(8,128)S(1)}, s32[16,1,128]{2,1,0:T(1,128)S(1)}, s32[8,512]{1,0:T(8,128)S(1)}) custom-call(s32[1,8,256]{2,1,0:T(8,128)S(1)} %copy-done.6, s32[1,2,128]{2,1,0:T(2,128)S(1)} %copy-done.5), custom_call_target="tpu_custom_call" | custom-call | tf_op jit(solution)/shard_map/lists/pallas_call | solution.py:613
  24.3 8.5 %render.2 = f32[16,16,128]{2,1,0:T(8,128)} custom-call(s32[1]{0:T(128)} %bitcast.4.tile_ref, f32[16,72,128]{2,1,0:T(8,128)S(1)} %bitcast.38, bf16[8,256,256]{2,1,0:T(8,128)(2,1)S(1)} %get-tuple-element.25.before_ref, f32[8,256]{1,0:T(8,128)S(1)} %get-tuple-element.26.live_ref, f32[1,8,3,256]{3,2,1,0:T(4,128)S(1)} %copy.15.goal_ref, ...), custom_call_target="tpu_custom_call" | custom-call | tf_op jit(solution)/shard_map/render/pallas_call | solution.py:658
  32.8 4.5 %all-to-all-start = ((f32[16,16,128]{2,1,0:T(8,128)}), f32[16,16,128]{2,1,0:T(8,128)S(1)}, u32[]{:S(2)}, u32[]{:S(2)}) async-start(f32[16,16,128]{2,1,0:T(8,128)} %render.2), calls=%async_computation | async-start | bytes 262144 | tf_op jit(solution)/shard_map/all_to_all | solution.py:626
  37.4 0.6 copy-done.9
  38.1 0.6 fusion.7
  40.1 6.0 %all-to-all-done.gmsg_ref = f32[16,16,128]{2,1,0:T(8,128)S(1)} async-done(((f32[16,16,128]{2,1,0:T(8,128)}), f32[16,16,128]{2,1,0:T(8,128)S(1)}, u32[]{:S(2)}, u32[]{:S(2)}) %all-to-all-start) | async-done | bytes 131104 | tf_op jit(solution)/shard_map/all_to_all | solution.py:626
  46.0 2.9 %update.2 = (f32[59,512]{1,0:T(8,128)S(1)}, f32[59,512]{1,0:T(8,128)S(1)}, f32[59,512]{1,0:T(8,128)S(1)}, f32[2,59,128]{2,1,0:T(8,128)S(1)}, f32[59,128]{1,0:T(8...) custom-call(f32[2]{0:T(128)S(1)} %get-tuple-element.48.w_ref, ...), custom_call_target="tpu_custom_call" | custom-call | tf_op jit(solution)/shard_map/update/pallas_call | solution.py:677
  48.9 3.5 %all-to-all-start.1 = ((f32[16,16,128]{2,1,0:T(8,128)}), f32[16,16,128]{2,1,0:T(8,128)S(1)}, u32[]{:S(2)}, u32[]{:S(2)}) async-start(f32[16,16,128]{2,1,0:T(8,128)} %get-tuple-element.29), calls=%async_computation.1 | async-start | bytes 262144 | tf_op jit(solution)/shard_map/all_to_all | solution.py:626
  52.5 5.4 %collective-permute-start = (f32[59,128]{1,0:T(8,128)S(1)}, f32[59,128]{1,0:T(8,128)S(1)}, u32[]{:S(2)}, u32[]{:S(2)}) collective-permute-start(f32[59,128]{1,0:T(8,128)S(1)} %get-tuple-element.35), channel_id=1, source_target_pairs={{0,16},{16,32},{32,48},{48,64},{64,80},{80,96},{96,112},{112,128},... | collective-permute-start | bytes 90632 | tf_op jit(solution)/shard_map/ppermute | solution.py:649
  57.9 1.9 %collective-permute-start.1 = (f32[59,128]{1,0:T(8,128)S(1)}, f32[59,128]{1,0:T(8,128)S(1)}, u32[]{:S(2)}, u32[]{:S(2)}) collective-permute-start(f32[59,128]{1,0:T(8,128)S(1)} %get-tuple-element.36), channel_id=1, source_target_pairs={{16,0},{32,16},{48,32},{64,48},{80,64},{96,80},{112,96},{128,112},... | collective-permute-start | bytes 90632 | tf_op jit(solution)/shard_map/ppermute | solution.py:649
  59.8 1.3 %all-to-all-done.1.msg_in = f32[16,16,128]{2,1,0:T(8,128)S(1)} async-done(((f32[16,16,128]{2,1,0:T(8,128)}), f32[16,16,128]{2,1,0:T(8,128)S(1)}, u32[]{:S(2)}, u32[]{:S(2)}) %all-to-all-start.1) | async-done | bytes 131104 | tf_op jit(solution)/shard_map/all_to_all | solution.py:626
  61.1 8.3 %render.3 = f32[16,16,128]{2,1,0:T(8,128)} custom-call(s32[1]{0:T(128)} %bitcast.4.tile_ref, f32[16,16,128]{2,1,0:T(8,128)S(1)} %all-to-all-done.1.msg_in, bf16[8,256,256]{2,1,0:T(8,128)(2,1)S(1)} %get-tuple-element.25.before_ref, f32[8,256]{1,0:T(8,128)S(1)} %get-tuple-element.26.live_ref, f32[1,8,3,256]{3,2,1,0:T(4,128)S(1)} %copy.15.goal_ref), custom_call_target="tpu_custom_call" | custom-call | tf_op jit(solution)/shard_map/render/pallas_call | solution.py:660
  69.3 5.9 %all-to-all-start.2 = ((f32[16,16,128]{2,1,0:T(8,128)}), f32[16,16,128]{2,1,0:T(8,128)S(1)}, u32[]{:S(2)}, u32[]{:S(2)}) async-start(f32[16,16,128]{2,1,0:T(8,128)} %render.3), calls=%async_computation.2 | async-start | bytes 262144 | tf_op jit(solution)/shard_map/all_to_all | solution.py:626
  75.2 0.1 fusion.5
  75.3 8.5 %all-to-all-done.2.gmsg_ref = f32[16,16,128]{2,1,0:T(8,128)S(1)} async-done(((f32[16,16,128]{2,1,0:T(8,128)}), f32[16,16,128]{2,1,0:T(8,128)S(1)}, u32[]{:S(2)}, u32[]{:S(2)}) %all-to-all-start.2) | async-done | bytes 131104 | tf_op jit(solution)/shard_map/all_to_all | solution.py:626
  83.9 2.6 %update.3 = (f32[59,512]{1,0:T(8,128)}, f32[59,512]{1,0:T(8,128)}, f32[59,512]{1,0:T(8,128)}, f32[2,59,128]{2,1,0:T(8,128)S(1)}, f32[59,128]{1,0:T(8,128)S(1)}, /*index=5*/f32[59,128]{1,0:T(8,128)S(1)}) custom-call(f32[2]{0:T(128)S(1)} %get-tuple-element.48.w_ref, f32[1,2,8]{2,1,0:T(2,128)S(1)} %copy-done.4, f32[16,16,128]{2,1,0:T(8,128)S(1)} %all-to-all-done.2.gmsg_ref, ...), custom_call_target="tpu_custom_call" | custom-call | tf_op jit(solution)/shard_map/update/pallas_call | solution.py:677
  86.4 7.2 %collective-permute-start.2 = (f32[59,128]{1,0:T(8,128)S(1)}, f32[59,128]{1,0:T(8,128)S(1)}, u32[]{:S(2)}, u32[]{:S(2)}) collective-permute-start(f32[59,128]{1,0:T(8,128)S(1)} %get-tuple-element.41), channel_id=1, source_target_pairs={{0,16},{16,32},{32,48},{48,64},{64,80},{80,96},{96,112},{112,128},... | collective-permute-start | bytes 90632 | tf_op jit(solution)/shard_map/ppermute | solution.py:649
  93.7 1.9 %collective-permute-start.3 = (f32[59,128]{1,0:T(8,128)S(1)}, f32[59,128]{1,0:T(8,128)S(1)}, u32[]{:S(2)}, u32[]{:S(2)}) collective-permute-start(f32[59,128]{1,0:T(8,128)S(1)} %get-tuple-element.42), channel_id=1, source_target_pairs={{16,0},{32,16},{48,32},{64,48},{80,64},{96,80},{112,96},{128,112},... | collective-permute-start | bytes 90632 | tf_op jit(solution)/shard_map/ppermute | solution.py:649
  95.6 7.2 %collective-permute-done.3.right_ref = f32[59,128]{1,0:T(8,128)S(1)} collective-permute-done((f32[59,128]{1,0:T(8,128)S(1)}, f32[59,128]{1,0:T(8,128)S(1)}, u32[]{:S(2)}, u32[]{:S(2)}) %collective-permute-start.3) | collective-permute-done | bytes 30240 | tf_op jit(solution)/shard_map/ppermute | solution.py:649
  102.8 1.3 %consensus.1 = (f32[59,2,128]{2,1,0:T(2,128)}, f32[59,2,128]{2,1,0:T(2,128)}) custom-call(f32[2]{0:T(128)S(1)} %get-tuple-element.48.w_ref, f32[2,59,128]{2,1,0:T(8,128)S(1)} %get-tuple-element.40.side_ref, f32[1,2,59,128]{3,2,1,0:T(8,128)S(1)} %get-tuple-element.45.rest_7_.u_ref, f32[59,128]{1,0:T(8,128)S(1)} %collective-permute-done.2.left_ref, ...), custom_call_target="tpu_custom_call" | custom-call | tf_op jit(solution)/shard_map/consensus/pallas_call | solution.py:708
  (25 shorter events, 0.1 us)
Async XLA Ops:
  0.6 0.8 copy-start.4
  1.4 0.9 copy-start
  3.0 19.2 %copy-start.5 = (s32[1,2,128]{2,1,0:T(2,128)S(1)}, s32[1,2,128]{2,1,0:T(2,128)}, u32[]{:S(2)}) copy-start(s32[1,2,128]{2,1,0:T(2,128)} %rest_4_.1) | copy-start | bytes 3076
  3.0 19.2 %copy-start.6 = (s32[1,8,256]{2,1,0:T(8,128)S(1)}, s32[1,8,256]{2,1,0:T(8,128)}, u32[]{:S(2)}) copy-start(s32[1,8,256]{2,1,0:T(8,128)} %lists_ref.1) | copy-start | bytes 24580
  32.8 5.2 %copy-start.8 = (f32[1,2,59,128]{3,1,2,0:T(2,128)S(1)}, f32[1,2,59,128]{3,1,2,0:T(2,128)}, u32[]{:S(2)}) copy-start(f32[1,2,59,128]{3,1,2,0:T(2,128)} %param.18) | copy-start | bytes 181252
  32.8 5.3 %copy-start.7 = (f32[1,2,59,128]{3,1,2,0:T(2,128)S(1)}, f32[1,2,59,128]{3,1,2,0:T(2,128)}, u32[]{:S(2)}) copy-start(f32[1,2,59,128]{3,1,2,0:T(2,128)} %param.19) | copy-start | bytes 181252
  32.8 13.2 %copy-start.3 = (f32[59,512]{1,0:T(8,128)S(1)}, f32[59,512]{1,0:T(8,128)}, u32[]{:S(2)}) copy-start(f32[59,512]{1,0:T(8,128)} %rest_2_.1) | copy-start | bytes 362500
  32.8 13.2 %all-to-all-start = ((f32[16,16,128]{2,1,0:T(8,128)}), f32[16,16,128]{2,1,0:T(8,128)S(1)}, u32[]{:S(2)}, u32[]{:S(2)}) async-start(f32[16,16,128]{2,1,0:T(8,128)} %render.2), calls=%async_computation | async-start | bytes 262144 | tf_op jit(solution)/shard_map/all_to_all | solution.py:626
  37.4 0.7 copy-start.9
  38.1 8.0 %copy-start.1 = (f32[59,512]{1,0:T(8,128)S(1)}, f32[59,512]{1,0:T(8,128)}, u32[]{:S(2)}) copy-start(f32[59,512]{1,0:T(8,128)} %rest_0_.1) | copy-start | bytes 362500
  38.1 8.0 %copy-start.2 = (f32[59,512]{1,0:T(8,128)S(1)}, f32[59,512]{1,0:T(8,128)}, u32[]{:S(2)}) copy-start(f32[59,512]{1,0:T(8,128)} %rest_1_.1) | copy-start | bytes 362500
  48.9 12.1 %all-to-all-start.1 = ((f32[16,16,128]{2,1,0:T(8,128)}), f32[16,16,128]{2,1,0:T(8,128)S(1)}, u32[]{:S(2)}, u32[]{:S(2)}) async-start(f32[16,16,128]{2,1,0:T(8,128)} %get-tuple-element.29), calls=%async_computation.1 | async-start | bytes 262144 | tf_op jit(solution)/shard_map/all_to_all | solution.py:626
  52.5 22.8 %collective-permute-start = (f32[59,128]{1,0:T(8,128)S(1)}, f32[59,128]{1,0:T(8,128)S(1)}, u32[]{:S(2)}, u32[]{:S(2)}) collective-permute-start(f32[59,128]{1,0:T(8,128)S(1)} %get-tuple-element.35), channel_id=1, source_target_pairs={{0,16},{16,32},{32,48},{48,64},{64,80},{80,96},{96,112},{112,128},... | collective-permute-start | bytes 90632 | tf_op jit(solution)/shard_map/ppermute | solution.py:649
  57.9 17.4 %collective-permute-start.1 = (f32[59,128]{1,0:T(8,128)S(1)}, f32[59,128]{1,0:T(8,128)S(1)}, u32[]{:S(2)}, u32[]{:S(2)}) collective-permute-start(f32[59,128]{1,0:T(8,128)S(1)} %get-tuple-element.36), channel_id=1, source_target_pairs={{16,0},{32,16},{48,32},{64,48},{80,64},{96,80},{112,96},{128,112},... | collective-permute-start | bytes 90632 | tf_op jit(solution)/shard_map/ppermute | solution.py:649
  69.3 14.5 %all-to-all-start.2 = ((f32[16,16,128]{2,1,0:T(8,128)}), f32[16,16,128]{2,1,0:T(8,128)S(1)}, u32[]{:S(2)}, u32[]{:S(2)}) async-start(f32[16,16,128]{2,1,0:T(8,128)} %render.3), calls=%async_computation.2 | async-start | bytes 262144 | tf_op jit(solution)/shard_map/all_to_all | solution.py:626
  86.4 9.2 %collective-permute-start.2 = (f32[59,128]{1,0:T(8,128)S(1)}, f32[59,128]{1,0:T(8,128)S(1)}, u32[]{:S(2)}, u32[]{:S(2)}) collective-permute-start(f32[59,128]{1,0:T(8,128)S(1)} %get-tuple-element.41), channel_id=1, source_target_pairs={{0,16},{16,32},{32,48},{48,64},{64,80},{80,96},{96,112},{112,128},... | collective-permute-start | bytes 90632 | tf_op jit(solution)/shard_map/ppermute | solution.py:649
  93.7 9.1 %collective-permute-start.3 = (f32[59,128]{1,0:T(8,128)S(1)}, f32[59,128]{1,0:T(8,128)S(1)}, u32[]{:S(2)}, u32[]{:S(2)}) collective-permute-start(f32[59,128]{1,0:T(8,128)S(1)} %get-tuple-element.42), channel_id=1, source_target_pairs={{16,0},{32,16},{48,32},{64,48},{80,64},{96,80},{112,96},{128,112},... | collective-permute-start | bytes 90632 | tf_op jit(solution)/shard_map/ppermute | solution.py:649

commit v2 on v1

--- a/solution.py
+++ b/solution.py
@@ -18,7 +18,8 @@
 ROWS = 16
 FEATS = 9
 WIDE = 72
-TOGETHER = 2
+BUFS = 2
+CHUNK = 256
 GRANT = 10 << 20
 
 sh_zero = 0.28209479177387814
@@ -281,9 +282,35 @@
     inv_ref[...] = total.astype(i32) - 1
 
 
-def features_kernel(centre_y, x_ref, cam_ref, feat_ref, wide):
-    spread(x_ref, wide)
-    make_features(wide, camera_of(cam_ref), centre_y, feat_ref)
+def start_kernel(
+    centre_y,
+    lists_hbm,
+    bidx_hbm,
+    x_hbm,
+    cam_hbm,
+    feat_ref,
+    before_ref,
+    live_ref,
+    req_ref,
+    inv_ref,
+    lists,
+    bidx,
+    x,
+    cam,
+    wide,
+    sems,
+):
+    pairs = ((lists_hbm, lists), (bidx_hbm, bidx), (x_hbm, x), (cam_hbm, cam))
+    copies = [pltpu.make_async_copy(a, b, sems.at[i]) for i, (a, b) in enumerate(pairs)]
+    for copy in copies:
+        copy.start()
+    copies[0].wait()
+    copies[1].wait()
+    lists_kernel(lists, bidx, before_ref, live_ref, req_ref, inv_ref)
+    copies[2].wait()
+    copies[3].wait()
+    spread(x, wide)
+    make_features(wide, camera_of(cam), centre_y, feat_ref)
 
 
 def render_kernel(
@@ -302,20 +329,23 @@
             main, last = pick_features(
                 sources_of(lambda rows: msg_in[o, rows, :]), msg_in[o, 64:72, :], req_ref[o]
             )
-            msg_ref[o, 0:8, :] = main
-            msg_ref[o, 8:9, :] = last
-            out_ref[o, 9:10, :] = req_ref[o].astype(f32)
+            msg_ref[ROWS * o : ROWS * o + 8, :] = main
+            msg_ref[ROWS * o + 8 : ROWS * o + 9, :] = last
+            out_ref[10 * o + 9 : 10 * o + 10, :] = req_ref[o].astype(f32)
     else:
         msg_ref, out_ref = msg_in, rest[0]
         rest = rest[1:]
+    rows_in = ROWS if first_round else FEATS
+    rows_out = FEATS + first_round
     feat, grad, grad8, goal8, alpha, lk_h, lk_l, wgt, wgt_h, wgt_l, u_f, u_h, u_l = rest
     row = iota((8, 128), 0)
     col = iota((8, 128), 1)
     block = col >> 4
     inner = col & (CAP - 1)
     for h in range(2):
-        whole = [msg_ref[8 * h + o, 0:8, :] for o in range(8)]
-        ninth = jnp.concatenate([msg_ref[8 * h + o, 8:9, :] for o in range(8)], axis=0)
+        starts = [rows_in * (8 * h + o) for o in range(8)]
+        whole = [msg_ref[at : at + 8, :] for at in starts]
+        ninth = jnp.concatenate([msg_ref[at + 8 : at + 9, :] for at in starts], axis=0)
         for l in range(LISTS):
             got = whole[l]
             for o in range(8):
@@ -329,95 +359,112 @@
     sub16 = iota((16, SLOTS), 0).astype(f32)
     row8 = iota((8, SLOTS), 0)
     half = -0.5 * log2e
-    group = range(TOGETHER)
     down = functools.partial(jnp.sum, axis=0, keepdims=True)
-
-    def some_lists(step, carry):
-        lists = [step * TOGETHER + i for i in group]
-        f8, opac, off_x, start_y, mean_y, quad_a, quad_b, prec_y = ([None] * TOGETHER for _ in range(8))
-        for i, l in enumerate(lists):
-            number = tile * SCREENS + lax.rem(l, SCREENS)
-            start_x = (16 * lax.rem(number, 8)).astype(f32) + 0.5
-            start_y[i] = (16 * lax.div(number, 8)).astype(f32) + 0.5
-            f8[i] = feat[l, 0:8, :]
-            opac[i] = feat[l, 8:9, :] * live_ref[pl.ds(l, 1), :]
-            off_x[i] = (sub16 + start_x) - f8[i][3:4, :]
-            quad_a[i] = (half * f8[i][5:6, :]) * off_x[i] * off_x[i]
-            quad_b[i] = (2.0 * half * f8[i][6:7, :]) * off_x[i]
-            prec_y[i] = half * f8[i][7:8, :]
-            mean_y[i] = f8[i][4:5, :]
-        for y in range(16):
-            rows = slice(16 * y, 16 * y + 16)
-            for i in group:
-                off_y = (start_y[i] + float(y)) - mean_y[i]
-                quad = quad_a[i] + (off_y * quad_b[i] + prec_y[i] * off_y * off_y)
-                a = opac[i] * jnp.exp2(quad)
+    state = [None] * LISTS
+
+    def front(l):
+        b = l % BUFS
+        number = tile * SCREENS + l % SCREENS
+        start_x = (16 * lax.rem(number, 8)).astype(f32) + 0.5
+        start_y = (16 * lax.div(number, 8)).astype(f32) + 0.5
+        f8 = feat[l, 0:8, :]
+        opac = feat[l, 8:9, :] * live_ref[l : l + 1, :]
+        off_x = (sub16 + start_x) - f8[3:4, :]
+        quad_a = (half * f8[5:6, :]) * off_x * off_x
+        quad_b = (2.0 * half * f8[6:7, :]) * off_x
+        prec_y = half * f8[7:8, :]
+        mean_y = f8[4:5, :]
+        state[l] = (f8, off_x, start_y, mean_y)
+        for at in range(0, SLOTS, CHUNK):
+            for y in range(at // 16, (at + CHUNK) // 16):
+                rows = slice(16 * y, 16 * y + 16)
+                off_y = (start_y + float(y)) - mean_y
+                quad = quad_a + (off_y * quad_b + prec_y * off_y * off_y)
+                a = opac * jnp.exp2(quad)
                 high, low = split(jnp.log(1.0 - a))
-                alpha[i, rows, :] = a
-                lk_h[i, rows, :] = high
-                lk_l[i, rows, :] = low
-        before = [before_ref[l] for l in lists]
-        for c in range(4):
-            rows = slice(64 * c, 64 * c + 64)
-            for i in group:
-                total = dot(lk_h[i, rows, :], before[i]) + dot(lk_l[i, rows, :], before[i])
-                w = jnp.exp2(total * log2e) * alpha[i, rows, :]
+                alpha[b, rows, :] = a
+                lk_h[b, rows, :] = high
+                lk_l[b, rows, :] = low
+                if y % 4 == 3:
+                    yield
+            rows = slice(at, at + CHUNK)
+            before = before_ref[l]
+            total = dot(lk_h[b, rows, :], before) + dot(lk_l[b, rows, :], before)
+            for sub in range(0, CHUNK, 32):
+                rows = slice(at + sub, at + sub + 32)
+                w = jnp.exp2(total[sub : sub + 32] * log2e) * alpha[b, rows, :]
                 high, low = split(w)
-                wgt[i, rows, :] = w
-                wgt_h[i, rows, :] = high
-                wgt_l[i, rows, :] = low
-        left, right, d_h, d_l = ([None] * TOGETHER for _ in range(4))
-        for i, l in enumerate(lists):
-            c_h, c_l = split(f8[i])
-            image = dot_t(c_h, wgt_h[i]) + (dot_t(c_h, wgt_l[i]) + dot_t(c_l, wgt_h[i]))
-            goal8[i, 0:3, :] = goal_ref[0, l]
-            diff = jnp.where(row8 < 3, image - goal8[i], 0.0)
-            d_h[i], d_l[i] = split(diff)
-            d_hf = d_h[i].astype(f32)
-            d_lf = d_l[i].astype(f32)
-            c_hf = c_h.astype(f32)
-            c_lf = c_l.astype(f32)
-            left[i] = jnp.transpose(jnp.concatenate([d_hf, d_hf, d_lf, d_lf], axis=0)).astype(bf16)
-            right[i] = jnp.concatenate([c_hf, c_lf, c_hf, c_lf], axis=0).astype(bf16)
-        for c in range(4):
-            rows = slice(64 * c, 64 * c + 64)
-            for i in group:
-                u = wgt[i, rows, :] * dot(left[i][rows, :], right[i])
+                wgt[b, rows, :] = w
+                wgt_h[b, rows, :] = high
+                wgt_l[b, rows, :] = low
+            yield
+
+    def back(l):
+        b = l % BUFS
+        f8, off_x, start_y, mean_y = state[l]
+        c_h, c_l = split(f8)
+        c_hf = c_h.astype(f32)
+        c_lf = c_l.astype(f32)
+        c_both = jnp.concatenate([c_hf, c_lf], axis=0).astype(bf16)
+        image = dot_t(c_both, wgt_h[b])
+        image = image[0:8] + (image[8:16] + dot_t(c_h, wgt_l[b]))
+        yield
+        for ch in range(3):
+            goal8[b, ch : ch + 1, :] = goal_ref[0, ch, l : l + 1, :]
+        diff = jnp.where(row8 < 3, image - goal8[b], 0.0)
+        d_h, d_l = split(diff)
+        d_hf = d_h.astype(f32)
+        d_lf = d_l.astype(f32)
+        d_both = jnp.concatenate([d_hf, d_lf], axis=0).astype(bf16)
+        left = jnp.transpose(jnp.concatenate([d_hf, d_hf, d_lf, d_lf], axis=0)).astype(bf16)
+        right = jnp.concatenate([c_hf, c_lf, c_hf, c_lf], axis=0).astype(bf16)
+        yield
+        sums = [jnp.zeros((16, SLOTS), f32) for _ in range(3)]
+        before = before_ref[l]
+        for at in range(0, SLOTS, CHUNK):
+            slopes = dot(left[at : at + CHUNK], right)
+            for sub in range(0, CHUNK, 32):
+                rows = slice(at + sub, at + sub + 32)
+                u = wgt[b, rows, :] * slopes[sub : sub + 32]
                 high, low = split(u)
-                u_f[i, rows, :] = u
-                u_h[i, rows, :] = high
-                u_l[i, rows, :] = low
-        sums = [[jnp.zeros((16, SLOTS), f32) for _ in range(3)] for _ in group]
-        for c in range(4):
-            rows = slice(64 * c, 64 * c + 64)
-            for i in group:
-                later = dot_t(u_h[i, rows, :], before[i]) + dot_t(u_l[i, rows, :], before[i])
-                a = alpha[i, rows, :]
-                slope = u_f[i, rows, :] - later * (a / (1.0 - a))
-                for y in range(4):
-                    off_y = (start_y[i] + float(4 * c + y)) - mean_y[i]
-                    part = slope[16 * y : 16 * y + 16, :]
-                    moved = off_y * part
-                    sums[i][0] = sums[i][0] + part
-                    sums[i][1] = sums[i][1] + moved
-                    sums[i][2] = sums[i][2] + off_y * moved
-        for i, l in enumerate(lists):
-            colour = dot(d_h[i], wgt_h[i]) + (dot(d_h[i], wgt_l[i]) + dot(d_l[i], wgt_h[i]))
-            by_x = sums[i][0] * off_x[i]
-            moments = (
-                down(sums[i][0]),
-                down(by_x),
-                down(sums[i][1]),
-                down(by_x * off_x[i]),
-                down(sums[i][1] * off_x[i]),
-            )
-            for j in range(5):
-                colour = jnp.where(row8 == 3 + j, moments[j], colour)
-            grad[l] = colour
-            grad8[pl.ds(l, 1), :] = down(sums[i][2])
-        return carry
-
-    lax.fori_loop(0, LISTS // TOGETHER, some_lists, 0)
+                u_f[b, rows, :] = u
+                u_h[b, rows, :] = high
+                u_l[b, rows, :] = low
+            yield
+            rows = slice(at, at + CHUNK)
+            later = dot_t(u_h[b, rows, :], before) + dot_t(u_l[b, rows, :], before)
+            for sub in range(0, CHUNK, 16):
+                rows = slice(at + sub, at + sub + 16)
+                a = alpha[b, rows, :]
+                part = u_f[b, rows, :] - later[sub : sub + 16] * (a / (1.0 - a))
+                off_y = (start_y + float((at + sub) // 16)) - mean_y
+                moved = off_y * part
+                sums[0] = sums[0] + part
+                sums[1] = sums[1] + moved
+                sums[2] = sums[2] + off_y * moved
+                if sub % 64 == 48:
+                    yield
+        colour = dot(d_both, wgt_h[b])
+        colour = colour[0:8] + (colour[8:16] + dot(d_h, wgt_l[b]))
+        by_x = sums[0] * off_x
+        moments = (
+            down(sums[0]),
+            down(by_x),
+            down(sums[1]),
+            down(by_x * off_x),
+            down(sums[1] * off_x),
+        )
+        for i in range(5):
+            colour = jnp.where(row8 == 3 + i, moments[i], colour)
+        grad[l] = colour
+        grad8[l : l + 1, :] = down(sums[2])
+        yield
+
+    for l in range(LISTS + 1):
+        streams = ([back(l - 1)] if l > 0 else []) + ([front(l)] if l < LISTS else [])
+        while streams:
+            streams = [stream for stream in streams if next(stream, streams) is None]
+
     for h in range(2):
         lanes = slice(128 * h, 128 * (h + 1))
         whole = [grad[l, :, lanes] for l in range(LISTS)]
@@ -427,9 +474,10 @@
             for l in range(LISTS):
                 if l != o:
                     got = jnp.where(block == l, pltpu.roll(whole[l], (l - o) * CAP % 128, 1), got)
-            out_ref[8 * h + o, 0:8, :] = got
+            at = rows_out * (8 * h + o)
+            out_ref[at : at + 8, :] = got
             last = jnp.where(row == block, lane_gather(ninth, inner + CAP * o), 0.0)
-            out_ref[8 * h + o, 8:9, :] = jnp.sum(last, axis=0, keepdims=True)
+            out_ref[at + 8 : at + 9, :] = jnp.sum(last, axis=0, keepdims=True)
 
 
 def side_columns(x_ref, bidx_ref, a, e):
@@ -440,6 +488,19 @@
     return jnp.where(
         part < 2, jnp.where(part == 0, got[0], got[1]), jnp.where(part == 2, got[2], got[3])
     )
+
+
+def adam(step, g, x, m, v):
+    m = beta_one * m + (1.0 - beta_one) * g
+    v = beta_two * v + (1.0 - beta_two) * g * g
+    corr_one = 1.0 - beta_one**step
+    corr_two = 1.0 - beta_two**step
+    x = x - (learn_rate / corr_one) * m / (jnp.sqrt(v * (1.0 / corr_two)) + adam_eps)
+    return x, m, v
+
+
+def adam_kernel(step, g_ref, x_ref, m_ref, v_ref, xo_ref, mo_ref, vo_ref):
+    xo_ref[...], mo_ref[...], vo_ref[...] = adam(step, g_ref[...], x_ref[...], m_ref[...], v_ref[...])
 
 
 def update_kernel(
@@ -454,16 +515,23 @@
     if last_round:
         req_ref, *rest = rest
     (x_ref, m_ref, v_ref, bidx_ref, inv_ref, z_ref, u_ref), rest = rest[:7], rest[7:]
-    (xo_ref, mo_ref, vo_ref, side_ref, sh0_ref, sh1_ref), rest = rest[:6], rest[6:]
+    if last_round:
+        g_ref, *rest = rest
+    else:
+        (xo_ref, mo_ref, vo_ref), rest = rest[:3], rest[3:]
+    (side_ref, near_ref, far_ref), rest = rest[:3], rest[3:]
     if last_round:
         wide, gin, gwide, terms, hits, prox, pad, grad = rest
     else:
         msg_ref, req_out, wide, feat, gin, gwide, terms, hits, prox, pad, grad = rest
+    rows_in = FEATS if last_round else FEATS + 1
     first = iota((ROWS, 128), 1) < 64
     sub_n = iota((SPL, 128), 0)
     for t in range(TILES):
         lanes = slice(128 * t, 128 * (t + 1))
-        high, low = split(gmsg_ref[t])
+        at = rows_in * t
+        ninth = jnp.broadcast_to(gmsg_ref[at + 8 : at + 9, :], (8, 128))
+        high, low = split(jnp.concatenate([gmsg_ref[at : at + 8, :], ninth], axis=0))
         zero = jnp.zeros_like(high)
         terms[0:16, lanes] = jnp.where(first, high, zero)
         terms[16:32, lanes] = jnp.where(first, zero, high)
@@ -472,7 +540,7 @@
         if last_round:
             wanted = req_ref[t]
         else:
-            wanted = gmsg_ref[t, 9:10, :].astype(i32)
+            wanted = gmsg_ref[at + 9 : at + 10, :].astype(i32)
             req_out[t] = wanted
         hits[:, lanes] = jnp.where(wanted == sub_n, 1.0, 0.0).astype(bf16)
     found = dot_t(terms[...], hits[...])
@@ -536,39 +604,47 @@
                 + gwide[pl.ds(8 * a + 4 + k, 8, stride=8), :]
                 + jnp.where(inverse >= 0, add, 0.0)
             )
-    g = grad[0:PARAMS, :]
-    m = beta_one * m_ref[...] + (1.0 - beta_one) * g
-    v = beta_two * v_ref[...] + (1.0 - beta_two) * g * g
-    corr_one = 1.0 - beta_one**step
-    corr_two = 1.0 - beta_two**step
-    x = x_ref[...] - (learn_rate / corr_one) * m / (jnp.sqrt(v * (1.0 / corr_two)) + adam_eps)
-    mo_ref[...] = m
-    vo_ref[...] = v
-    xo_ref[...] = x
+    x, m, v = adam(step, grad[0:PARAMS, :], x_ref[...], m_ref[...], v_ref[...])
+    if last_round:
+        g_ref[...] = grad[0:PARAMS, :]
+    else:
+        xo_ref[...] = x
+        mo_ref[...] = m
+        vo_ref[...] = v
     pad[0:PARAMS, :] = x
+    even = w_ref[2] > 0.5
     for a in range(0, PARAMS, 8):
         n = min(8, PARAMS - a)
+        shared = []
         for e in range(2):
             mine = side_columns(pad, bidx_ref, a, e)[0:n]
             side_ref[e, a : a + n, :] = mine
-            (sh0_ref, sh1_ref)[e][a : a + n, :] = mine + u_ref[0, e, a : a + n, :]
+            shared.append(mine + u_ref[0, e, a : a + n, :])
+        near_ref[a : a + n, :] = jnp.where(even, shared[1], shared[0])
+        far_ref[a : a + n, :] = jnp.where(even, shared[0], shared[1])
     if not last_round:
         spread(pad, wide)
         make_features(wide, cam, centre_y, feat)
         sources = sources_of(lambda rows: feat[rows, :])
         opac = feat[64:72, :]
         for t in range(TILES):
-            main, last = pick_features(sources, opac, gmsg_ref[t, 9:10, :].astype(i32))
-            msg_ref[t, 0:8, :] = main
-            msg_ref[t, 8:9, :] = last
-
-
-def consensus_kernel(w_ref, side_ref, u_ref, left_ref, right_ref, zo_ref, uo_ref):
+            main, last = pick_features(
+                sources, opac, gmsg_ref[rows_in * t + 9 : rows_in * t + 10, :].astype(i32)
+            )
+            msg_ref[FEATS * t : FEATS * t + 8, :] = main
+            msg_ref[FEATS * t + 8 : FEATS * t + 9, :] = last
+
+
+def consensus_kernel(w_ref, side_ref, u_ref, near_ref, far_ref, zo_ref, uo_ref):
+    even = w_ref[2] > 0.5
+    near = near_ref[...]
+    far = far_ref[...]
+    partner = (jnp.where(even, far, near), jnp.where(even, near, far))
     for e in range(2):
         w = w_ref[e]
         own = side_ref[e]
         dual = u_ref[0, e]
-        agreed = w * (own + dual + (left_ref, right_ref)[e][...]) * 0.5 + (1.0 - w) * own
+        agreed = w * (own + dual + partner[e]) * 0.5 + (1.0 - w) * own
         zo_ref[:, e, :] = agreed
         uo_ref[:, e, :] = dual + w * (own - agreed)
 
@@ -587,10 +663,12 @@
     link_vals = links.astype(f32)
     right_w = jnp.where(block_idx < block_total - 1, link_vals[block_idx], 0.0)
     left_w = jnp.where(block_idx > 0, link_vals[jnp.maximum(block_idx - 1, 0)], 0.0)
-    side_w = jnp.stack([left_w, right_w])
+    even = block_idx % 2 == 0
+    side_w = jnp.stack([left_w, right_w, jnp.where(even, 1.0, 0.0)])
+    goals = jnp.transpose(targets, (0, 2, 1, 3))
     tile_num = tile_idx.astype(i32).reshape(1)
 
-    def call(kernel, name, outs, ins, scratch=()):
+    def call(kernel, outs, ins, scratch=()):
         return pl.pallas_call(
             kernel,
             out_shape=outs,
@@ -598,55 +676,55 @@
             out_specs=jax.tree.map(lambda _: ANY_VMEM, outs),
             scratch_shapes=list(scratch),
             compiler_params=pltpu.CompilerParams(vmem_limit_bytes=GRANT),
-            name=name,
         )
 
     wide_scratch = VMEM((512, 128), f32)
-    features = call(
-        functools.partial(features_kernel, centre_y),
-        "features",
-        shape((WIDE, 128)),
-        [ANY_VMEM, ANY_SMEM],
-        [wide_scratch],
-    )(params, cameras)
-    message = lax.all_gather(features, "tile")
-    before, live, wanted, inverse = call(
-        lists_kernel,
-        "lists",
+    features, before, live, wanted, inverse = call(
+        functools.partial(start_kernel, centre_y),
         (
+            shape((WIDE, 128)),
             shape((LISTS, SLOTS, SLOTS), bf16),
             shape((LISTS, SLOTS)),
             shape((TILES, 1, 128), i32),
             shape((8, SPL), i32),
         ),
-        [ANY_VMEM] * 2,
-    )(tile_lists, boundary_index)
-
-    def exchange(value):
-        return lax.all_to_all(value, "tile", 0, 0, tiled=True)
+        [pl.BlockSpec(memory_space=pltpu.HBM)] * 4,
+        [
+            VMEM((1, LISTS, SLOTS), i32),
+            VMEM((1, 2, NB), i32),
+            VMEM((PARAMS, SPL), f32),
+            pltpu.SMEM((1, 2, 8), f32),
+            wide_scratch,
+            pltpu.SemaphoreType.DMA((4,)),
+        ],
+    )(tile_lists, boundary_index, params, cameras)
+    message = lax.all_gather(features, "tile")
+
+    def exchange(value, rows):
+        moved = lax.all_to_all(value.reshape(TILES, 1, rows * 128), "tile", 0, 0, tiled=True)
+        return moved.reshape(TILES * rows, 128)
 
     def render(first_round):
         scratch = [
             VMEM((LISTS, 16, SLOTS), f32),
             VMEM((LISTS, 8, SLOTS), f32),
             VMEM((LISTS, SLOTS), f32),
-            VMEM((TOGETHER, 8, SLOTS), f32),
+            VMEM((BUFS, 8, SLOTS), f32),
         ]
         for kind in (f32, bf16, bf16, f32, bf16, bf16, f32, bf16, bf16):
-            scratch.append(VMEM((TOGETHER, SLOTS, SLOTS), kind))
+            scratch.append(VMEM((BUFS, SLOTS, SLOTS), kind))
         if first_round:
-            scratch.append(VMEM((TILES, ROWS, 128), f32))
+            scratch.append(VMEM((TILES * ROWS, 128), f32))
         return call(
             functools.partial(render_kernel, first_round),
-            "render",
-            shape((TILES, ROWS, 128)),
+            shape((TILES * (FEATS + first_round), 128)),
             [ANY_SMEM] + [ANY_VMEM] * (5 if first_round else 4),
             scratch,
         )
 
-    def shifted(x, by):
-        pairs = [(i, i + by) for i in range(block_total) if 0 <= i + by < block_total]
-        return lax.ppermute(x, "block", pairs)
+    def swapped(x, first):
+        pairs = [(i, i + 1) for i in range(first, block_total - 1, 2)]
+        return lax.ppermute(x, "block", pairs + [(j, i) for i, j in pairs])
 
     values, moment_one, moment_two = params, moment1, moment2
     agreed, dual_vars = consensus, duals
@@ -655,14 +733,16 @@
         last_round = round_idx == ROUNDS - 1
         first_round = round_idx == 0
         if first_round:
-            sent = render(True)(tile_num, message, before, live, targets, wanted)
+            sent = render(True)(tile_num, message, before, live, goals, wanted)
         else:
-            sent = render(False)(tile_num, exchange(message), before, live, targets)
-        back = exchange(sent)
-        outs = [shape((PARAMS, SPL))] * 3 + [shape((2, PARAMS, NB))] + [shape((PARAMS, NB))] * 2
+            received = exchange(message, FEATS)
+            sent = render(False)(tile_num, received, before, live, goals)
+        back = exchange(sent, FEATS + first_round)
+        outs = [shape((PARAMS, SPL))] * (1 if last_round else 3)
+        outs += [shape((2, PARAMS, NB))] + [shape((PARAMS, NB))] * 2
         scratch = [wide_scratch]
         if not last_round:
-            outs += [shape((TILES, ROWS, 128)), shape((TILES, 1, 128), i32)]
+            outs += [shape((TILES * FEATS, 128)), shape((TILES, 1, 128), i32)]
             scratch += [VMEM((WIDE, 128), f32)]
         scratch += [
             VMEM((WIDE, 128), f32),
@@ -676,7 +756,6 @@
         known = (requests,) if last_round else ()
         outs = call(
             functools.partial(update_kernel, first_step + round_idx + 1, last_round, centre_y),
-            "update",
             tuple(outs),
             [ANY_SMEM, ANY_SMEM] + [ANY_VMEM] * (8 + len(known)),
             scratch,
@@ -693,20 +772,28 @@
             agreed,
             dual_vars,
         )
-        values, moment_one, moment_two, own_sides, shared0, shared1 = outs[:6]
-        from_left = shifted(shared1, 1)
-        from_right = shifted(shared0, -1)
+        if last_round:
+            grads, own_sides, near, far = outs
+        else:
+            *changed, own_sides, near, far, message, requests = outs
+        far = swapped(far, 1)
+        near = swapped(near, 0)
         if not last_round:
-            message, requests = outs[6:]
-            partner = jnp.stack([from_left, from_right])[None]
+            values, moment_one, moment_two = changed
+            partner = jnp.stack([jnp.where(even, far, near), jnp.where(even, near, far)])[None]
             own_sides = own_sides[None]
-            wide_w = side_w[None, :, None, None]
+            wide_w = side_w[None, :2, None, None]
             agreed = wide_w * (own_sides + dual_vars + partner) * 0.5 + (1.0 - wide_w) * own_sides
             dual_vars = dual_vars + wide_w * (own_sides - agreed)
         else:
+            values, moment_one, moment_two = call(
+                functools.partial(adam_kernel, first_step + ROUNDS),
+                (shape((PARAMS, SPL)),) * 3,
+                [ANY_VMEM] * 4,
+            )(grads, values, moment_one, moment_two)
             sides = (shape((PARAMS, 2, NB)),) * 2
-            sides = call(consensus_kernel, "consensus", sides, [ANY_SMEM] + [ANY_VMEM] * 4)(
-                side_w, own_sides, dual_vars, from_left, from_right
+            sides = call(consensus_kernel, sides, [ANY_SMEM] + [ANY_VMEM] * 4)(
+                side_w, own_sides, dual_vars, near, far
             )
             agreed, dual_vars = (jnp.transpose(side, (1, 0, 2))[None] for side in sides)
     return (values, moment_one, moment_two, agreed, dual_vars)

time: 105 us -> 99.2 us (0.945)
  Pallas kernels: 26.2 us -> 21.5 us
  starting transfers between devices: 30.4 us -> 26.7 us
  waiting for transfers between devices: 23 us -> 25.2 us
    all_to_all x3, waiting for transfers between devices: 15.8 us -> 20.6 us  [exchange(): lax.all_to_all(value.reshape(TILES, 1, rows * 128), 'tile', 0, 0, tiled=T...]
    pallas_call x5, Pallas kernels: 20.8 us -> 16.7 us  [the longest x1 6.18 us: on_device(): sent = render(True)(tile_num, message, before, live, goals, wanted)]
    ppermute x4, waiting for transfers between devices: 7.2 us -> 4.65 us  [swapped(): return lax.ppermute(x, 'block', pairs + [(j, i) for i, j in pairs])]
    all_to_all x3, starting transfers between devices: 13.9 us -> 11.7 us  [exchange(): lax.all_to_all(value.reshape(TILES, 1, rows * 128), 'tile', 0, 0, tiled=T...]
    ppermute x4, starting transfers between devices: 16.5 us -> 15 us  [swapped(): return lax.ppermute(x, 'block', pairs + [(j, i) for i, j in pairs])]
    unnamed x23 -> x24, local copies, waits for them, and re-layouts: 2.35 us -> 2.97 us
  transfers between devices with their start and end apart: 7 -> 7, of which waited for: 4 -> 5; matrix products, arithmetic and copies ran while one was open for 1% -> 1% of each run, Pallas kernels for 8% -> 1%
where the time goes in v2:
time: 99.2 us; the launch traced here: 98.7 us
  starting transfers between devices  26.7 us (27%)
  waiting for transfers between devices  25.2 us (25%)
  Pallas kernels  21.5 us (22%)
  blocking collectives  19.2 us (19%)
  local copies, waits for them, and re-layouts  3.56 us (4%)
  between operations  2.13 us (2%)
    all_to_all x3, waiting for transfers between devices, exchange(): lax.all_to_all(value.reshape(TILES, 1, rows * 128), 'tile', 0, 0, tiled=T...  20.6 us
    all_gather x1, blocking collectives, on_device(): message = lax.all_gather(features, 'tile')  19.2 us
    ppermute x4, starting transfers between devices, swapped(): return lax.ppermute(x, 'block', pairs + [(j, i) for i, j in pairs])  15 us
    all_to_all x3, starting transfers between devices, exchange(): lax.all_to_all(value.reshape(TILES, 1, rows * 128), 'tile', 0, 0, tiled=T...  11.7 us
    pallas_call x1, Pallas kernels, on_device(): sent = render(True)(tile_num, message, before, live, goals, wanted)  6.18 us
    pallas_call x1, Pallas kernels, on_device(): sent = render(False)(tile_num, received, before, live, goals)  6.04 us
    pallas_call x2, Pallas kernels, on_device(): call(functools.partial(update_kernel, first_step + round_idx + 1, last_ro...  4.81 us
    ppermute x4, waiting for transfers between devices, swapped(): return lax.ppermute(x, 'block', pairs + [(j, i) for i, j in pairs])  4.65 us
  transfers between devices with their start and end apart: 7, of which 5 were waited for; matrix products, arithmetic and copies ran while one was open for 1% of the time, Pallas kernels for 1%

profile of v2, /device:TPU:198, one launch (start us, length us, event | category | flops | bytes accessed | tf_op | source)
XLA Modules:
  0.0 98.7 jit_solution(573750778572789926)
XLA Ops:
  0.7 0.7 copy-done.6
  1.3 0.9 copy-done
  2.2 0.7 copy-done.7
  2.9 2.4 %shard_map.137 = (f32[72,128]{1,0:T(8,128)S(1)}, bf16[8,256,256]{2,1,0:T(8,128)(2,1)S(1)}, f32[8,256]{1,0:T(8,128)S(1)}, s32[16,1,128]{2,1,0:T(1,128)S(1)}, s32[8,512]{1,0:T(8,128)S(1)}) custom-call(s32[1,8,256]{2,1,0:T(8,128)S(1)} %copy-done.7, s32[1,2,128]{2,1,0:T(2,128)S(1)} %copy-done.6, f32[59,512]{1,0:T(8,128)S(1)} %copy-done, f32[1,2,8]{2,1,0:T(2,128)S(1)} %copy-done.5), custom_call_target="tpu_custom_call" | custom-call | tf_op jit(solution)/shard_map/pallas_call | solution.py:682
  5.4 19.2 %all-gather = f32[1152,128]{1,0:T(8,128)S(1)} all-gather(f32[72,128]{1,0:T(8,128)S(1)} %get-tuple-element.27), channel_id=2, replica_groups=mesh['block'=32,'tile'=16] {'tile'}, dimensions={0}, use_global_device_ids=true | all-gather | bytes 626688 | tf_op jit(solution)/shard_map/all_gather | solution.py:701
  24.6 6.2 %shard_map.138 = f32[160,128]{1,0:T(8,128)} custom-call(s32[1]{0:T(128)} %bitcast.5.tile_ref, f32[16,72,128]{2,1,0:T(8,128)S(1)} %bitcast.48, bf16[8,256,256]{2,1,0:T(8,128)(2,1)S(1)} %get-tuple-element.28.before_ref, f32[8,256]{1,0:T(8,128)S(1)} %get-tuple-element.29.live_ref, f32[1,3,8,256]{3,2,1,0:T(8,128)S(1)} %bitcast.52, ...), custom_call_target="tpu_custom_call" | custom-call | tf_op jit(solution)/shard_map/pallas_call | solution.py:736
  30.8 4.5 %all-to-all-start = ((f32[16,1,1280]{2,1,0:T(1,128)}), f32[16,1,1280]{2,1,0:T(1,128)S(1)}, u32[]{:S(2)}, u32[]{:S(2)}) async-start(f32[16,1,1280]{2,1,0:T(1,128)} %bitcast.8), calls=%async_computation | async-start | bytes 163840 | tf_op jit(solution)/shard_map/all_to_all | solution.py:704
  35.4 0.6 copy-done.10
  36.1 0.6 fusion.7
  38.1 5.3 %all-to-all-done = f32[16,1,1280]{2,1,0:T(1,128)S(1)} async-done(((f32[16,1,1280]{2,1,0:T(1,128)}), f32[16,1,1280]{2,1,0:T(1,128)S(1)}, u32[]{:S(2)}, u32[]{:S(2)}) %all-to-all-start) | async-done | bytes 81952 | tf_op jit(solution)/shard_map/all_to_all | solution.py:704
  43.4 2.9 %shard_map.139 = (f32[59,512]{1,0:T(8,128)S(1)}, f32[59,512]{1,0:T(8,128)S(1)}, f32[59,512]{1,0:T(8,128)S(1)}, f32[2,59,128]{2,1,0:T(8,128)S(1)}, f32[59,128]{1,...) custom-call(f32[3]{0:T(128)S(1)} %pad_maximum_fusion.w_ref, ...), custom_call_target="tpu_custom_call" | custom-call | tf_op jit(solution)/shard_map/pallas_call | solution.py:757
  46.2 5.4 %collective-permute-start = (f32[59,128]{1,0:T(8,128)S(1)}, f32[59,128]{1,0:T(8,128)S(1)}, u32[]{:S(2)}, u32[]{:S(2)}) collective-permute-start(f32[59,128]{1,0:T(8,128)S(1)} %get-tuple-element.38), channel_id=1, source_target_pairs={{16,32},{48,64},{80,96},{112,128},{144,160},{176,192},{208,224},{2... | collective-permute-start | bytes 90632 | tf_op jit(solution)/shard_map/ppermute | solution.py:727
  51.6 1.9 %collective-permute-start.1 = (f32[59,128]{1,0:T(8,128)S(1)}, f32[59,128]{1,0:T(8,128)S(1)}, u32[]{:S(2)}, u32[]{:S(2)}) collective-permute-start(f32[59,128]{1,0:T(8,128)S(1)} %get-tuple-element.39), channel_id=1, source_target_pairs={{0,16},{32,48},{64,80},{96,112},{128,144},{160,176},{192,208},{224... | collective-permute-start | bytes 90632 | tf_op jit(solution)/shard_map/ppermute | solution.py:727
  53.6 3.7 %all-to-all-start.1 = ((f32[16,1,1152]{2,1,0:T(1,128)}), f32[16,1,1152]{2,1,0:T(1,128)S(1)}, u32[]{:S(2)}, u32[]{:S(2)}) async-start(f32[16,1,1152]{2,1,0:T(1,128)} %bitcast.10), calls=%async_computation.1 | async-start | bytes 147456 | tf_op jit(solution)/shard_map/all_to_all | solution.py:704
  57.5 7.5 %all-to-all-done.1 = f32[16,1,1152]{2,1,0:T(1,128)S(1)} async-done(((f32[16,1,1152]{2,1,0:T(1,128)}), f32[16,1,1152]{2,1,0:T(1,128)S(1)}, u32[]{:S(2)}, u32[]{:S(2)}) %all-to-all-start.1) | async-done | bytes 73760 | tf_op jit(solution)/shard_map/all_to_all | solution.py:704
  65.0 6.0 %shard_map.140 = f32[144,128]{1,0:T(8,128)} custom-call(s32[1]{0:T(128)} %bitcast.5.tile_ref, f32[144,128]{1,0:T(8,128)S(1)} %bitcast.50, bf16[8,256,256]{2,1,0:T(8,128)(2,1)S(1)} %get-tuple-element.28.before_ref, f32[8,256]{1,0:T(8,128)S(1)} %get-tuple-element.29.live_ref, f32[1,3,8,256]{3,2,1,0:T(8,128)S(1)} %bitcast.53), custom_call_target="tpu_custom_call" | custom-call | tf_op jit(solution)/shard_map/pallas_call | solution.py:739
  71.0 3.5 %all-to-all-start.2 = ((f32[16,1,1152]{2,1,0:T(1,128)}), f32[16,1,1152]{2,1,0:T(1,128)S(1)}, u32[]{:S(2)}, u32[]{:S(2)}) async-start(f32[16,1,1152]{2,1,0:T(1,128)} %bitcast.12), calls=%async_computation.2 | async-start | bytes 147456 | tf_op jit(solution)/shard_map/all_to_all | solution.py:704
  74.6 7.8 %all-to-all-done.2 = f32[16,1,1152]{2,1,0:T(1,128)S(1)} async-done(((f32[16,1,1152]{2,1,0:T(1,128)}), f32[16,1,1152]{2,1,0:T(1,128)S(1)}, u32[]{:S(2)}, u32[]{:S(2)}) %all-to-all-start.2) | async-done | bytes 73760 | tf_op jit(solution)/shard_map/all_to_all | solution.py:704
  82.4 1.9 %shard_map.141 = (f32[59,512]{1,0:T(8,128)S(1)}, f32[2,59,128]{2,1,0:T(8,128)S(1)}, f32[59,128]{1,0:T(8,128)S(1)}, f32[59,128]{1,0:T(8,128)S(1)}) custom-call(f32[3]{0:T(128)S(1)} %pad_maximum_fusion.w_ref, f32[1,2,8]{2,1,0:T(2,128)S(1)} %copy-done.5, f32[144,128]{1,0:T(8,128)S(1)} %bitcast.51, s32[16,1,128]{2,1,0:T(1,128)S(1)} %get-tuple-element.33.rest_0_, ...), custom_call_target="tpu_custom_call" | custom-call | tf_op jit(solution)/shard_map/pallas_call | solution.py:757
  84.4 3.9 %collective-permute-start.2 = (f32[59,128]{1,0:T(8,128)S(1)}, f32[59,128]{1,0:T(8,128)S(1)}, u32[]{:S(2)}, u32[]{:S(2)}) collective-permute-start(f32[59,128]{1,0:T(8,128)S(1)} %get-tuple-element.45), channel_id=1, source_target_pairs={{0,16},{32,48},{64,80},{96,112},{128,144},{160,176},{192,208},{224... | collective-permute-start | bytes 90632 | tf_op jit(solution)/shard_map/ppermute | solution.py:727
  88.3 3.8 %collective-permute-start.3 = (f32[59,128]{1,0:T(8,128)S(1)}, f32[59,128]{1,0:T(8,128)S(1)}, u32[]{:S(2)}, u32[]{:S(2)}) collective-permute-start(f32[59,128]{1,0:T(8,128)S(1)} %get-tuple-element.46), channel_id=1, source_target_pairs={{16,32},{48,64},{80,96},{112,128},{144,160},{176,192},{208,224},{2... | collective-permute-start | bytes 90632 | tf_op jit(solution)/shard_map/ppermute | solution.py:727
  92.1 0.8 shard_map.142
  92.9 4.5 %collective-permute-done.3.far_ref = f32[59,128]{1,0:T(8,128)S(1)} collective-permute-done((f32[59,128]{1,0:T(8,128)S(1)}, f32[59,128]{1,0:T(8,128)S(1)}, u32[]{:S(2)}, u32[]{:S(2)}) %collective-permute-start.3) | collective-permute-done | bytes 30240 | tf_op jit(solution)/shard_map/ppermute | solution.py:727
  97.4 1.3 %shard_map.143 = (f32[59,2,128]{2,1,0:T(2,128)}, f32[59,2,128]{2,1,0:T(2,128)}) custom-call(f32[3]{0:T(128)S(1)} %pad_maximum_fusion.w_ref, f32[2,59,128]{2,1,0:T(8,128)S(1)} %get-tuple-element.44.side_ref, f32[1,2,59,128]{3,2,1,0:T(8,128)S(1)} %get-tuple-element.49.rest_7_.u_ref, f32[59,128]{1,0:T(8,128)S(1)} %collective-permute-done.2.near_ref, ...), custom_call_target="tpu_custom_call" | custom-call | tf_op jit(solution)/shard_map/pallas_call | solution.py:795
  (28 shorter events, 0.4 us)
Async XLA Ops:
  0.6 0.7 copy-start.6
  0.6 0.7 copy-start.5
  1.3 0.9 copy-start
  2.2 0.7 copy-start.7
  5.4 19.2 %copy-start.4 = (f32[1,8,3,256]{3,1,2,0:T(8,128)S(1)}, f32[1,8,3,256]{3,1,2,0:T(8,128)}, u32[]{:S(2)}) copy-start(f32[1,8,3,256]{3,1,2,0:T(8,128)} %param.15) | copy-start | bytes 73732
  24.6 11.4 %copy-start.9 = (f32[1,2,59,128]{3,1,2,0:T(2,128)S(1)}, f32[1,2,59,128]{3,1,2,0:T(2,128)}, u32[]{:S(2)}) copy-start(f32[1,2,59,128]{3,1,2,0:T(2,128)} %param.18) | copy-start | bytes 181252
  30.8 5.3 %copy-start.8 = (f32[1,2,59,128]{3,1,2,0:T(2,128)S(1)}, f32[1,2,59,128]{3,1,2,0:T(2,128)}, u32[]{:S(2)}) copy-start(f32[1,2,59,128]{3,1,2,0:T(2,128)} %param.19) | copy-start | bytes 181252
  30.8 12.6 %copy-start.3 = (f32[59,512]{1,0:T(8,128)S(1)}, f32[59,512]{1,0:T(8,128)}, u32[]{:S(2)}) copy-start(f32[59,512]{1,0:T(8,128)} %rest_2_.1) | copy-start | bytes 362500
  30.8 12.6 %all-to-all-start = ((f32[16,1,1280]{2,1,0:T(1,128)}), f32[16,1,1280]{2,1,0:T(1,128)S(1)}, u32[]{:S(2)}, u32[]{:S(2)}) async-start(f32[16,1,1280]{2,1,0:T(1,128)} %bitcast.8), calls=%async_computation | async-start | bytes 163840 | tf_op jit(solution)/shard_map/all_to_all | solution.py:704
  35.4 0.7 copy-start.10
  36.0 7.3 %copy-start.1 = (f32[59,512]{1,0:T(8,128)S(1)}, f32[59,512]{1,0:T(8,128)}, u32[]{:S(2)}) copy-start(f32[59,512]{1,0:T(8,128)} %rest_0_.1) | copy-start | bytes 362500
  36.0 7.3 %copy-start.2 = (f32[59,512]{1,0:T(8,128)S(1)}, f32[59,512]{1,0:T(8,128)}, u32[]{:S(2)}) copy-start(f32[59,512]{1,0:T(8,128)} %rest_1_.1) | copy-start | bytes 362500
  46.2 11.1 %collective-permute-start = (f32[59,128]{1,0:T(8,128)S(1)}, f32[59,128]{1,0:T(8,128)S(1)}, u32[]{:S(2)}, u32[]{:S(2)}) collective-permute-start(f32[59,128]{1,0:T(8,128)S(1)} %get-tuple-element.38), channel_id=1, source_target_pairs={{16,32},{48,64},{80,96},{112,128},{144,160},{176,192},{208,224},{2... | collective-permute-start | bytes 90632 | tf_op jit(solution)/shard_map/ppermute | solution.py:727
  51.6 5.8 %collective-permute-start.1 = (f32[59,128]{1,0:T(8,128)S(1)}, f32[59,128]{1,0:T(8,128)S(1)}, u32[]{:S(2)}, u32[]{:S(2)}) collective-permute-start(f32[59,128]{1,0:T(8,128)S(1)} %get-tuple-element.39), channel_id=1, source_target_pairs={{0,16},{32,48},{64,80},{96,112},{128,144},{160,176},{192,208},{224... | collective-permute-start | bytes 90632 | tf_op jit(solution)/shard_map/ppermute | solution.py:727
  53.6 11.4 %all-to-all-start.1 = ((f32[16,1,1152]{2,1,0:T(1,128)}), f32[16,1,1152]{2,1,0:T(1,128)S(1)}, u32[]{:S(2)}, u32[]{:S(2)}) async-start(f32[16,1,1152]{2,1,0:T(1,128)} %bitcast.10), calls=%async_computation.1 | async-start | bytes 147456 | tf_op jit(solution)/shard_map/all_to_all | solution.py:704
  71.0 11.4 %all-to-all-start.2 = ((f32[16,1,1152]{2,1,0:T(1,128)}), f32[16,1,1152]{2,1,0:T(1,128)S(1)}, u32[]{:S(2)}, u32[]{:S(2)}) async-start(f32[16,1,1152]{2,1,0:T(1,128)} %bitcast.12), calls=%async_computation.2 | async-start | bytes 147456 | tf_op jit(solution)/shard_map/all_to_all | solution.py:704
  84.4 8.5 %collective-permute-start.2 = (f32[59,128]{1,0:T(8,128)S(1)}, f32[59,128]{1,0:T(8,128)S(1)}, u32[]{:S(2)}, u32[]{:S(2)}) collective-permute-start(f32[59,128]{1,0:T(8,128)S(1)} %get-tuple-element.45), channel_id=1, source_target_pairs={{0,16},{32,48},{64,80},{96,112},{128,144},{160,176},{192,208},{224... | collective-permute-start | bytes 90632 | tf_op jit(solution)/shard_map/ppermute | solution.py:727
  88.3 9.1 %collective-permute-start.3 = (f32[59,128]{1,0:T(8,128)S(1)}, f32[59,128]{1,0:T(8,128)S(1)}, u32[]{:S(2)}, u32[]{:S(2)}) collective-permute-start(f32[59,128]{1,0:T(8,128)S(1)} %get-tuple-element.46), channel_id=1, source_target_pairs={{16,32},{48,64},{80,96},{112,128},{144,160},{176,192},{208,224},{2... | collective-permute-start | bytes 90632 | tf_op jit(solution)/shard_map/ppermute | solution.py:727
